TPU v7x, 32 devices: a whole 2x2x4 slice. The times are simulated.
32 devices in a mesh: pb: 2 (over x), row: 16 (over z, y, core).
Axes of the slice: x: 2, y: 2, z: 4, core: 2. Of those that a mesh axis runs over, the one named last changes fastest.
Arguments:
- force_constants: float32 [9, 4608, 4608], P(None, 'row', 'pb'), may hold values from -0.1 to 3.6, as said below
- offsets: int32 [9, 3], replicated, may hold values from -2 to 2, as said below
- qpoints: int32 [2, 3], replicated, may hold values from 0 to 7
- lower_bound: float32 [2], P('pb'), may hold values from 1.5 to 2.5
- upper_bound: float32 [2], P('pb'), may hold values from 5.5 to 6.5
- start_vectors: float32 [4608, 128], P('row'), may hold values from -6 to 6
Outputs:
- basis: float32 [2, 4608, 128], P('pb', 'row')
- ritz: float32 [2, 64, 128], P('pb')
Inputs may be any that keep to these rules, and one draw needn't show every extreme that they name: `force_constants`: cell 0 is symmetric; for 1 <= c <= 4, cell c + 4 is the transpose of cell c, so every D(q) is Hermitian. `offsets`: row 0 is zero; for 1 <= c <= 4, row c + 4 is the negative of row c.
All inputs are finite; a program needn't handle non-finite values.
Results may differ from a plain program's by a relative error of at most 0.00025.
Values sent between devices are 32-bit elements; how exact they have to be, the bound alone decides.
A program may use at most 128 MiB of HBM per device.

v0:
```python
import functools
import math

import jax
import jax.numpy as jnp
from jax import lax
from jax.experimental import pallas as pl
from jax.experimental.pallas import tpu as pltpu
from jax.sharding import PartitionSpec as P

MODES = 4608
QDEN = 8


highest = lax.Precision.HIGHEST


def product(left, right):
    return jnp.dot(left, right, precision=highest, preferred_element_type=jnp.float32)


def inner_product(left, right):
    return lax.dot_general(
        left, right, (((0,), (0,)), ((), ())), precision=highest, preferred_element_type=jnp.float32
    )


def complex_times(left_real, left_imag, right_real, right_imag):
    return (
        product(left_real, right_real) - product(left_imag, right_imag),
        product(left_real, right_imag) + product(left_imag, right_real),
    )


def phase_table(qpoints, offsets):
    turns = jnp.sum(qpoints[:, None, :] * offsets[None, :, :], axis=2)
    turns = jnp.mod(turns, QDEN)
    angle = 2.0 * math.pi / QDEN * turns.astype(jnp.float32)
    return jnp.stack([jnp.cos(angle), jnp.sin(angle)], axis=1)


def factor_inverse(gram_real, gram_imag):
    order_size = gram_real.shape[0]
    embedded = jnp.stack(
        [jnp.stack([gram_real, -gram_imag], axis=2), jnp.stack([gram_imag, gram_real], axis=2)],
        axis=1,
    ).reshape(2 * order_size, 2 * order_size)
    lower_factor = jnp.linalg.cholesky(embedded)
    identity = jnp.eye(2 * order_size, dtype=gram_real.dtype)
    inverse = jax.scipy.linalg.solve_triangular(lower_factor, identity, lower=True)
    blocks = inverse.reshape(order_size, 2, order_size, 2)
    return (blocks[:, 0, :, 0], blocks[:, 1, :, 0])


def right_block(inverse_real, inverse_imag):
    upper_half = jnp.concatenate([inverse_real.T, -inverse_imag.T], axis=1)
    lower_half = jnp.concatenate([inverse_imag.T, inverse_real.T], axis=1)
    return jnp.concatenate([upper_half, lower_half], axis=0)


def split_gram(matrix, vector_count):
    return (
        matrix[:vector_count, :vector_count] + matrix[vector_count:, vector_count:],
        matrix[:vector_count, vector_count:] - matrix[vector_count:, :vector_count],
    )


def combine_parts(part_real, part_imag, vector_count):
    return jnp.concatenate(
        [
            part_real[:, :vector_count] - part_imag[:, vector_count:],
            part_real[:, vector_count:] + part_imag[:, :vector_count],
        ],
        axis=1,
    )


def chebyshev(vectors, apply_matrix, lower_value, upper_value, first_image):
    centre = 0.5 * (upper_value + lower_value)
    spread = 0.5 * (upper_value - lower_value)
    previous = vectors
    first_image = apply_matrix(vectors)
    current = (first_image - centre * vectors) / spread
    following = 2.0 * (apply_matrix(current) - centre * current) / spread - previous
    previous, current = (current, following)
    return current


def on_device(force_constants, offsets, qpoints, lower_bound, upper_bound, start_vectors):
    cell_count, row_count, col_count = force_constants.shape
    qcount = qpoints.shape[0]
    vector_count = start_vectors.shape[1] // 2
    coefficients = phase_table(qpoints, offsets).reshape(2 * qcount, cell_count)
    partial_value = product(
        coefficients, force_constants.reshape(cell_count, row_count * col_count)
    )
    partial_value = partial_value.reshape(qcount, 2, row_count, col_count)
    owned_block = lax.all_to_all(partial_value, "pb", split_axis=0, concat_axis=3, tiled=True)
    dyn_real = owned_block[0, 0]
    dyn_imag = owned_block[0, 1]

    def accumulate(piece):
        return combine_parts(product(dyn_real, piece), product(dyn_imag, piece), vector_count)

    def apply_matrix(vectors):
        return accumulate(lax.all_gather(vectors, "row", axis=0, tiled=True))

    lower_value = lower_bound[0]
    upper_value = upper_bound[0]
    first_pass = chebyshev(start_vectors, apply_matrix, lower_value, upper_value, None)
    final_pass = chebyshev(first_pass, apply_matrix, lower_value, upper_value, None)
    image = apply_matrix(final_pass)
    over_total, proj_total = lax.psum(
        (inner_product(final_pass, final_pass), inner_product(final_pass, image)), "row"
    )
    over_real, over_imag = split_gram(over_total, vector_count)
    proj_real, proj_imag = split_gram(proj_total, vector_count)
    inverse_real, inverse_imag = factor_inverse(over_real, over_imag)
    basis_local = math.sqrt(MODES) * product(final_pass, right_block(inverse_real, inverse_imag))
    temp_real, temp_imag = complex_times(proj_real, proj_imag, inverse_real.T, -inverse_imag.T)
    ritz_real, ritz_imag = complex_times(inverse_real, inverse_imag, temp_real, temp_imag)
    ritz_local = jnp.concatenate([ritz_real, ritz_imag], axis=1)
    return (basis_local[None], ritz_local[None])


STEPS = 5
PIECES = 2
MESH = pl.DeviceIdType.MESH


def assemble_kernel(coef_ref, force_ref, high_ref, low_ref):
    cells, tile_rows, cols = force_ref.shape
    pairs = (cells - 1) // 2
    points = high_ref.shape[0]
    width = 256
    for at in range(cols // width):
        span = slice(at * width, (at + 1) * width)
        home = force_ref[0, :, span]
        real = [coef_ref[2 * q, 0] * home for q in range(points)]
        imag = [coef_ref[2 * q + 1, 0] * home for q in range(points)]
        for c in range(1, pairs + 1):
            first = force_ref[c, :, span]
            second = force_ref[c + pairs, :, span]
            total, difference = first + second, first - second
            for q in range(points):
                real[q] = real[q] + coef_ref[2 * q, c] * total
                imag[q] = imag[q] + coef_ref[2 * q + 1, c] * difference
        for q in range(points):
            for part, value in ((0, real[q]), (1, imag[q])):
                high = value.astype(jnp.bfloat16)
                high_ref[q, part, :, span] = high
                low_ref[q, part, :, span] = (value - high.astype(jnp.float32)).astype(jnp.bfloat16)


def assemble(coefficients, force_constants, points):
    cells, rows, cols = force_constants.shape
    tile = 48
    shape = jax.ShapeDtypeStruct((points, 2, rows, cols), jnp.bfloat16)
    block = pl.BlockSpec((points, 2, tile, cols), lambda i: (0, 0, i, 0))
    return pl.pallas_call(
        assemble_kernel,
        grid=(rows // tile,),
        out_shape=(shape, shape),
        in_specs=[
            pl.BlockSpec(memory_space=pltpu.SMEM),
            pl.BlockSpec((cells, tile, cols), lambda i: (0, i, 0)),
        ],
        out_specs=(block, block),
    )(coefficients, force_constants)


def sign_row(first, second):
    lane = lax.broadcasted_iota(jnp.int32, (1, 128), 1)
    return jnp.where(lane < 64, first, second).astype(jnp.float32)


def filter_kernel(
    bounds_ref, start_ref, high_ref, low_ref, final_ref, gram_ref,
    full, part, other, split, partner_bounds, sums, arrived,
    send_sem, recv_sem, x_send, x_recv, b_sem, g_send, g_recv,
):
    p = lax.axis_index("pb")
    row = lax.axis_index("row")
    rows = start_ref.shape[0]
    z, y, c = row // 4, (row // 2) % 2, row % 2
    position = z + p * (3 - 2 * z)
    owner = position < 2
    not_owner = position >= 2
    to_x = (1 - p, row)
    to_c = (p, row + 1 - 2 * c)
    to_y = (p, row + 2 - 4 * y)
    to_a = (p, row + 4 - 8 * (z % 2))
    to_b = (p, (3 - z) * 4 + y * 2 + c)
    near, far = 1 - p, p
    is_zero = jnp.where(position == 0, 1, 0)
    first = near + is_zero * (far - near)
    second = 1 - first
    mine = (z % 2) * 4 + y * 2 + c

    barrier = pltpu.get_barrier_semaphore()
    for target in (to_x, to_c, to_y, to_a, to_b):
        pl.semaphore_signal(barrier, inc=1, device_id=target, device_id_type=MESH)
    pl.semaphore_wait(barrier, 5)

    bound_copy = pltpu.make_async_remote_copy(
        src_ref=bounds_ref, dst_ref=partner_bounds, send_sem=b_sem.at[0], recv_sem=b_sem.at[1],
        device_id=to_x, device_id_type=MESH,
    )
    bound_copy.start()

    def block_rows(index):
        return pl.ds(pl.multiple_of(index * rows, 8), rows)

    @pl.when(owner)
    def _():
        full[0, 0, block_rows(mine), :] = start_ref[...]
        full[0, 1, block_rows(mine), :] = start_ref[...]

    bound_copy.wait()

    depth = rows // PIECES

    def send(slot, q, index, piece, lane, target):
        where = pl.ds(pl.multiple_of(index * rows + piece * depth, 8), depth)
        view = full.at[slot, q, where]
        return pltpu.make_async_remote_copy(
            src_ref=view, dst_ref=view, send_sem=send_sem.at[q, lane, piece],
            recv_sem=recv_sem.at[slot, q, index, piece], device_id=target, device_id_type=MESH,
        )

    def lane_block(level, flipped_y, flipped_c):
        yy = 1 - y if flipped_y else y
        cc = 1 - c if flipped_c else c
        return level * 4 + yy * 2 + cc

    def head_sends(slot, q, piece):
        index = lane_block(first, False, False)
        return (
            (position == 1, send(slot, q, index, piece, 1, to_b)),
            (position <= 2, send(slot, q, index, piece, 0, to_a)),
            (None, send(slot, q, index, piece, 2, to_y)),
            (None, send(slot, q, index, piece, 3, to_c)),
        )

    def tail_sends(slot, q, piece):
        index = lane_block(second, False, False)
        return (
            (position == 1, send(slot, q, index, piece, 5, to_b)),
            (position == 2, send(slot, q, index, piece, 4, to_a)),
            (None, send(slot, q, index, piece, 6, to_y)),
            (None, send(slot, q, index, piece, 7, to_c)),
        )

    def across_send(slot, q, piece, which):
        index = lane_block((first, second)[which], True, False)
        return send(slot, q, index, piece, 8 + which, to_c)

    def guarded(condition, action):
        if condition is None:
            action()
        else:
            pl.when(condition)(action)

    def await_block(slot, q, index, piece):
        send(slot, q, index, piece, 0, to_c).wait_recv()

    def head(slot, q, relay):
        for piece in range(PIECES):
            if relay:
                await_block(slot, q, lane_block(first, False, False), piece)
            for condition, copy in head_sends(slot, q, piece):
                guarded(condition, copy.start)

    def tail(slot, q):
        for piece in range(PIECES):
            await_block(slot, q, lane_block(second, False, False), piece)
            for condition, copy in tail_sends(slot, q, piece):
                guarded(condition, copy.start)

    def across(slot, q):
        for which in (0, 1):
            for piece in range(PIECES):
                await_block(slot, q, lane_block((first, second)[which], True, False), piece)
                across_send(slot, q, piece, which).start()

    def collect(slot, q):
        for flipped in (False, True):
            for level in (first, second):
                for piece in range(PIECES):
                    await_block(slot, q, lane_block(level, flipped, True), piece)

    def gathered(slot, q):
        across(slot, q)
        collect(slot, q)

    def await_sends(slot, q):
        for piece in range(PIECES):
            for condition, copy in head_sends(slot, q, piece) + tail_sends(slot, q, piece):
                guarded(condition, copy.wait_send)
            for which in (0, 1):
                across_send(slot, q, piece, which).wait_send()

    def partial_copy(slot, q):
        return pltpu.make_async_remote_copy(
            src_ref=part.at[q], dst_ref=other.at[slot, q], send_sem=x_send.at[q],
            recv_sem=x_recv.at[slot, q], device_id=to_x, device_id_type=MESH,
        )

    def final_copy(slot, q):
        return pltpu.make_async_remote_copy(
            src_ref=full.at[slot, q, block_rows(mine)], dst_ref=other.at[slot, q],
            send_sem=x_send.at[q], recv_sem=x_recv.at[slot, q],
            device_id=to_x, device_id_type=MESH,
        )

    def divide(slot, q):
        values = full[slot, q]
        upper = values.astype(jnp.bfloat16)
        split[:, :128] = upper
        split[:, 128:] = (values - upper.astype(jnp.float32)).astype(jnp.bfloat16)

    def multiply(q):
        def image(which):
            wide = jnp.dot(high_ref[q, which], split[...], preferred_element_type=jnp.float32)
            rest = jnp.dot(low_ref[q, which], split[:, :128], preferred_element_type=jnp.float32)
            return wide[:, :128] + (wide[:, 128:] + rest)
        part[q] = image(0) + sign_row(-1.0, 1.0) * pltpu.roll(image(1), 64, 1)

    def update(slot, q, weight, keep):
        own = jnp.where(p == q, 1.0, 0.0)
        centre = own * bounds_ref[0:1, :] + (1.0 - own) * partner_bounds[0:1, :]
        spread = own * bounds_ref[1:2, :] + (1.0 - own) * partner_bounds[1:2, :]
        current = full[slot, q, block_rows(mine), :]
        previous = full[1 - slot, q, block_rows(mine), :]
        image = part[q] + other[slot, q]
        full[1 - slot, q, block_rows(mine), :] = (
            weight * (image - centre * current) / spread - jnp.where(keep, previous, 0.0)
        )

    def step(k, carry):
        slot = k % 2
        later = k > 0
        middle = k < STEPS - 1
        weight = jnp.where(slot == 0, 1.0, 2.0)
        for q in (0, 1):
            if q == 0:
                gathered(slot, q)
                divide(slot, q)
            else:
                @pl.when(later)
                def _():
                    gathered(slot, q)
                    divide(slot, q)

            @pl.when(jnp.logical_and(later, not_owner))
            def _():
                partial_copy(1 - slot, q).wait_send()

            multiply(q)
            guarded(None if q == 0 else later, functools.partial(await_sends, slot, q))
            pl.when(jnp.logical_and(middle, not_owner))(partial_copy(slot, q).start)

            other_slot, other_q, ready = (slot, 1, later) if q == 0 else (1 - slot, 0, middle)
            pl.when(jnp.logical_and(ready, not_owner))(
                functools.partial(head, other_slot, other_q, True)
            )
            pl.when(ready)(functools.partial(tail, other_slot, other_q))

            @pl.when(jnp.logical_and(middle, owner))
            def _():
                partial_copy(slot, q).wait_recv()

                @pl.when(k == 0)
                def _():
                    full[1, q, block_rows(mine), :] = jnp.zeros((rows, 128), jnp.float32)

                update(slot, q, weight, slot == 1)
                head(1 - slot, q, False)

                @pl.when(k == STEPS - 2)
                def _():
                    final_copy(1 - slot, q).start()

        return carry

    pl.when(owner)(functools.partial(head, 0, 0, False))
    pl.when(not_owner)(functools.partial(head, 0, 0, True))
    tail(0, 0)
    lax.fori_loop(0, STEPS, step, 0)
    slot = (STEPS - 1) % 2

    @pl.when(owner)
    def _():
        for q in (0, 1):
            final_copy(slot, q).wait_send()
            other[slot, q] = full[slot, q, block_rows(mine), :]

    @pl.when(not_owner)
    def _():
        final_copy(slot, 0).wait_recv()
        final_copy(slot, 1).wait_recv()

    final_ref[...] = other[slot, p]

    def gram(left, right):
        whole = lax.dot_general(
            left, right, (((0,), (0,)), ((), ())), precision=highest,
            preferred_element_type=jnp.float32,
        )
        return whole[:64] + sign_row(1.0, -1.0) * pltpu.roll(whole[64:], 64, 1)

    sums[5, 0] = gram(other[slot, 1 - p], part[1 - p])
    cross = pltpu.make_async_remote_copy(
        src_ref=sums.at[5, 0], dst_ref=arrived.at[4, 0], send_sem=g_send.at[4],
        recv_sem=g_recv.at[4], device_id=to_x, device_id_type=MESH,
    )
    cross.start()
    sums[0, 0] = gram(other[slot, p], other[slot, p])
    own_projected = gram(other[slot, p], part[p])
    cross.wait()
    sums[0, 1] = own_projected + arrived[4, 0]
    for stage, target in enumerate((to_c, to_y, to_a, to_b)):
        copy = pltpu.make_async_remote_copy(
            src_ref=sums.at[stage], dst_ref=arrived.at[stage], send_sem=g_send.at[stage],
            recv_sem=g_recv.at[stage], device_id=target, device_id_type=MESH,
        )
        copy.start()
        copy.wait()
        sums[stage + 1] = sums[stage] + arrived[stage]
    gram_ref[...] = sums[4]


def filtered(bounds, start_vectors, high, low):
    rows = start_vectors.shape[0]
    points, _, _, cols = high.shape
    vmem = pl.BlockSpec(memory_space=pltpu.VMEM)
    dma = pltpu.SemaphoreType.DMA
    return pl.pallas_call(
        filter_kernel,
        out_shape=(
            jax.ShapeDtypeStruct((rows, 128), jnp.float32),
            jax.ShapeDtypeStruct((2, 64, 128), jnp.float32),
        ),
        in_specs=[vmem] * 4,
        out_specs=(vmem, vmem),
        scratch_shapes=[
            pltpu.VMEM((2, points, cols, 128), jnp.float32),
            pltpu.VMEM((points, rows, 128), jnp.float32),
            pltpu.VMEM((2, points, rows, 128), jnp.float32),
            pltpu.VMEM((cols, 256), jnp.bfloat16),
            pltpu.VMEM((8, 128), jnp.float32),
            pltpu.VMEM((6, 2, 64, 128), jnp.float32),
            pltpu.VMEM((5, 2, 64, 128), jnp.float32),
            dma((points, 10, PIECES)),
            dma((2, points, 8, PIECES)),
            dma((points,)),
            dma((2, points)),
            dma((2,)),
            dma((5,)),
            dma((5,)),
        ],
        compiler_params=pltpu.CompilerParams(
            collective_id=0, has_side_effects=True, vmem_limit_bytes=56 * 1024 * 1024
        ),
    )(bounds, start_vectors, high, low)


def finish_kernel(scale, final_ref, gram_ref, basis_ref, ritz_ref):
    size = gram_ref.shape[1]
    tile = 8
    gram = [gram_ref[0, t * tile:(t + 1) * tile, :] for t in range(size // tile)]
    lane = lax.broadcasted_iota(jnp.int32, (tile, 128), 1)
    line = lax.broadcasted_iota(jnp.int32, (tile, 128), 0)
    inverse = [jnp.where(lane == line + t * tile, 1.0, 0.0) for t in range(size // tile)]
    turn = sign_row(-1.0, 1.0)
    for j in range(size):
        home, at = j // tile, j % tile
        row = gram[home][at:at + 1, :]
        pivot = row[:, j:j + 1]
        row = row / pivot
        mate = inverse[home][at:at + 1, :] / pivot
        row_turned = turn * pltpu.roll(row, 64, 1)
        mate_turned = turn * pltpu.roll(mate, 64, 1)
        for t in range(home, size // tile):
            real = gram[t][:, j:j + 1]
            imag = gram[t][:, 64 + j:65 + j]
            if t == home:
                below = line[:, :1] > at
                real = jnp.where(below, real, 0.0)
                imag = jnp.where(below, imag, 0.0)
            gram[t] = gram[t] - (real * row + imag * row_turned)
            inverse[t] = inverse[t] - (real * mate + imag * mate_turned)
    scaled = []
    for t in range(size // tile):
        diagonal = jnp.sum(jnp.where(lane == line + t * tile, gram[t], 0.0), axis=1, keepdims=True)
        scaled.append(inverse[t] / jnp.sqrt(diagonal))
    whole = jnp.concatenate(scaled, axis=0)
    paired = jnp.concatenate([whole, turn * pltpu.roll(whole, 64, 1)], axis=0)

    def against(left):
        return lax.dot_general(
            left, paired, (((1,), (1,)), ((), ())), precision=highest,
            preferred_element_type=jnp.float32,
        )

    basis_ref[...] = scale * against(final_ref[...])
    half = against(gram_ref[1])
    ritz_ref[...] = product(whole, jnp.concatenate([half, turn * pltpu.roll(half, 64, 1)], axis=0))


def finish(final_pass, grams, modes):
    vmem = pl.BlockSpec(memory_space=pltpu.VMEM)
    return pl.pallas_call(
        functools.partial(finish_kernel, math.sqrt(modes)),
        out_shape=(
            jax.ShapeDtypeStruct(final_pass.shape, jnp.float32),
            jax.ShapeDtypeStruct(grams.shape[1:], jnp.float32),
        ),
        in_specs=[vmem] * 2,
        out_specs=(vmem, vmem),
    )(final_pass, grams)


def on_block(force_constants, offsets, qpoints, lower_bound, upper_bound, start_vectors):
    cell_count = force_constants.shape[0]
    qcount = qpoints.shape[0]
    coefficients = phase_table(qpoints, offsets).reshape(2 * qcount, cell_count)
    high, low = assemble(coefficients, force_constants, qcount)
    centre = 0.5 * (upper_bound + lower_bound)
    spread = 0.5 * (upper_bound - lower_bound)
    bounds = jnp.broadcast_to(
        jnp.concatenate([centre, spread, jnp.zeros((6,), jnp.float32)])[:, None], (8, 128)
    )
    final_pass, grams = filtered(bounds, start_vectors, high, low)
    basis_local, ritz_local = finish(final_pass, grams, MODES)
    return (basis_local[None], ritz_local[None])


def solution(mesh):
    paired = mesh.shape["pb"] == 2 and mesh.shape["row"] == 16
    return jax.shard_map(
        on_block if paired else on_device,
        mesh=mesh,
        in_specs=(P(None, "row", "pb"), P(), P(), P("pb"), P("pb"), P("row", None)),
        out_specs=(P("pb", "row", None), P("pb", None, None)),
        check_vma=False,
    )
```

profile of v0, /device:TPU:0, one launch (start us, length us, event | category | flops | bytes accessed | tf_op | source)
XLA Modules:
  0.0 179.5 jit_solution(10106848356669282069)
XLA Ops:
  1.9 0.1 pad_maximum_fusion.1
  2.0 0.8 copy.10
  2.8 0.8 multiply_reduce_fusion
  3.5 0.1 fusion.4
  3.6 0.6 copy.11
  4.2 0.7 broadcast_in_dim.6.bounds_ref
  4.9 14.3 %shard_map.77 = (bf16[2,2,288,2304]{3,2,1,0:T(8,128)(2,1)}, bf16[2,2,288,2304]{3,2,1,0:T(8,128)(2,1)}) custom-call(f32[4,9]{1,0:T(4,128)} %bitcast.9, f32[9,288,2304]{2,1,0:T(8,128)} %force_ref.1), custom_call_target="tpu_custom_call" | custom-call | tf_op jit(solution)/shard_map/pallas_call | solution.py:160
  19.2 148.2 %shard_map.78 = (f32[288,128]{1,0:T(8,128)}, f32[2,64,128]{2,1,0:T(8,128)}) custom-call(f32[8,128]{1,0:T(8,128)} %broadcast_in_dim.6.bounds_ref, f32[288,128]{1,0:T(8,128)} %start_ref.1, bf16[2,2,288,2304]{3,2,1,0:T(8,128)(2,1)} %get-tuple-element.8.high_ref, bf16[2,2,288,2304]{3,2,1,0:T(8,128)(2,1)} %get-tuple-element.9.low_ref), custom_call_target="tpu_custom_call" | custom-call | tf_op jit(solution)/shard_map/pallas_call | solution.py:438
  167.4 12.1 %shard_map.79 = (f32[288,128]{1,0:T(8,128)}, f32[64,128]{1,0:T(8,128)}) custom-call(f32[288,128]{1,0:T(8,128)} %get-tuple-element.10.final_ref, f32[2,64,128]{2,1,0:T(8,128)} %get-tuple-element.11.gram_ref), custom_call_target="tpu_custom_call" | custom-call | tf_op jit(solution)/shard_map/pallas_call | solution.py:513
  (2 shorter events, 0.0 us)
where the time goes:
time: 180 us
  Pallas kernels  175 us (97%)
  local copies, waits for them, and re-layouts  2.01 us (1%)
  between operations  1.95 us (1%)
    pallas_call x1, Pallas kernels, filtered(): pl.pallas_call(filter_kernel, out_shape=(jax.ShapeDtypeStruct((rows, 128)...  148 us
    pallas_call x1, Pallas kernels, assemble(): pl.pallas_call(assemble_kernel, grid=(rows // tile,), out_shape=(shape, s...  14.3 us
    pallas_call x1, Pallas kernels, finish(): pl.pallas_call(functools.partial(finish_kernel, math.sqrt(modes)), out_sh...  12.1 us

commit v1 on v0

v1 whole, which is shorter than its diff:
```python
import functools
import math

import jax
import jax.numpy as jnp
from jax import lax
from jax.experimental import pallas as pl
from jax.experimental.pallas import tpu as pltpu
from jax.sharding import PartitionSpec as P

MODES = 4608
QDEN = 8


highest = lax.Precision.HIGHEST


def product(left, right):
    return jnp.dot(left, right, precision=highest, preferred_element_type=jnp.float32)


def inner_product(left, right):
    return lax.dot_general(
        left, right, (((0,), (0,)), ((), ())), precision=highest, preferred_element_type=jnp.float32
    )


def complex_times(left_real, left_imag, right_real, right_imag):
    return (
        product(left_real, right_real) - product(left_imag, right_imag),
        product(left_real, right_imag) + product(left_imag, right_real),
    )


def phase_table(qpoints, offsets):
    turns = jnp.sum(qpoints[:, None, :] * offsets[None, :, :], axis=2)
    turns = jnp.mod(turns, QDEN)
    angle = 2.0 * math.pi / QDEN * turns.astype(jnp.float32)
    return jnp.stack([jnp.cos(angle), jnp.sin(angle)], axis=1)


def factor_inverse(gram_real, gram_imag):
    order_size = gram_real.shape[0]
    embedded = jnp.stack(
        [jnp.stack([gram_real, -gram_imag], axis=2), jnp.stack([gram_imag, gram_real], axis=2)],
        axis=1,
    ).reshape(2 * order_size, 2 * order_size)
    lower_factor = jnp.linalg.cholesky(embedded)
    identity = jnp.eye(2 * order_size, dtype=gram_real.dtype)
    inverse = jax.scipy.linalg.solve_triangular(lower_factor, identity, lower=True)
    blocks = inverse.reshape(order_size, 2, order_size, 2)
    return (blocks[:, 0, :, 0], blocks[:, 1, :, 0])


def right_block(inverse_real, inverse_imag):
    upper_half = jnp.concatenate([inverse_real.T, -inverse_imag.T], axis=1)
    lower_half = jnp.concatenate([inverse_imag.T, inverse_real.T], axis=1)
    return jnp.concatenate([upper_half, lower_half], axis=0)


def split_gram(matrix, vector_count):
    return (
        matrix[:vector_count, :vector_count] + matrix[vector_count:, vector_count:],
        matrix[:vector_count, vector_count:] - matrix[vector_count:, :vector_count],
    )


def combine_parts(part_real, part_imag, vector_count):
    return jnp.concatenate(
        [
            part_real[:, :vector_count] - part_imag[:, vector_count:],
            part_real[:, vector_count:] + part_imag[:, :vector_count],
        ],
        axis=1,
    )


def chebyshev(vectors, apply_matrix, lower_value, upper_value, first_image):
    centre = 0.5 * (upper_value + lower_value)
    spread = 0.5 * (upper_value - lower_value)
    previous = vectors
    first_image = apply_matrix(vectors)
    current = (first_image - centre * vectors) / spread
    following = 2.0 * (apply_matrix(current) - centre * current) / spread - previous
    previous, current = (current, following)
    return current


def on_device(force_constants, offsets, qpoints, lower_bound, upper_bound, start_vectors):
    cell_count, row_count, col_count = force_constants.shape
    qcount = qpoints.shape[0]
    vector_count = start_vectors.shape[1] // 2
    coefficients = phase_table(qpoints, offsets).reshape(2 * qcount, cell_count)
    partial_value = product(
        coefficients, force_constants.reshape(cell_count, row_count * col_count)
    )
    partial_value = partial_value.reshape(qcount, 2, row_count, col_count)
    owned_block = lax.all_to_all(partial_value, "pb", split_axis=0, concat_axis=3, tiled=True)
    dyn_real = owned_block[0, 0]
    dyn_imag = owned_block[0, 1]

    def accumulate(piece):
        return combine_parts(product(dyn_real, piece), product(dyn_imag, piece), vector_count)

    def apply_matrix(vectors):
        return accumulate(lax.all_gather(vectors, "row", axis=0, tiled=True))

    lower_value = lower_bound[0]
    upper_value = upper_bound[0]
    first_pass = chebyshev(start_vectors, apply_matrix, lower_value, upper_value, None)
    final_pass = chebyshev(first_pass, apply_matrix, lower_value, upper_value, None)
    image = apply_matrix(final_pass)
    over_total, proj_total = lax.psum(
        (inner_product(final_pass, final_pass), inner_product(final_pass, image)), "row"
    )
    over_real, over_imag = split_gram(over_total, vector_count)
    proj_real, proj_imag = split_gram(proj_total, vector_count)
    inverse_real, inverse_imag = factor_inverse(over_real, over_imag)
    basis_local = math.sqrt(MODES) * product(final_pass, right_block(inverse_real, inverse_imag))
    temp_real, temp_imag = complex_times(proj_real, proj_imag, inverse_real.T, -inverse_imag.T)
    ritz_real, ritz_imag = complex_times(inverse_real, inverse_imag, temp_real, temp_imag)
    ritz_local = jnp.concatenate([ritz_real, ritz_imag], axis=1)
    return (basis_local[None], ritz_local[None])


STEPS = 5
PIECES = 2
TILE = 48
FAR, NEAR, ACROSS_Y, ACROSS_C, RELAY_C = 0, 2, 3, 5, 7
KINDS = 9
MESH = pl.DeviceIdType.MESH


def sign_row(first, second):
    lane = lax.broadcasted_iota(jnp.int32, (1, 128), 1)
    return jnp.where(lane < 64, first, second).astype(jnp.float32)


def eighth_cosine(turn):
    turn = turn & (QDEN - 1)
    half = math.sqrt(0.5)
    value = jnp.float32(0.0)
    for index, exact in enumerate((1.0, half, 0.0, -half, -1.0, -half, 0.0, half)):
        value = jnp.where(turn == index, jnp.float32(exact), value)
    return value


def filter_kernel(
    offsets_ref, qpoints_ref, lower_ref, upper_ref, force_ref, start_ref, final_ref, gram_ref,
    tiles, high, low, full, own, part, other, split, bounds, partner_bounds, sums, arrived,
    tile_sem, send_sem, recv_sem, x_send, x_recv, b_sem, g_send, g_recv,
):
    p = lax.axis_index("pb")
    row = lax.axis_index("row")
    rows = start_ref.shape[0]
    cells = force_ref.shape[0]
    cols = force_ref.shape[2]
    pairs = (cells - 1) // 2
    points = 2
    depth = rows // PIECES
    z, y, c = row // 4, (row // 2) % 2, row % 2
    group = z // 2
    owner = group == p
    not_owner = group != p
    level = z % 2
    far_piece = group + p - 2 * group * p
    to_x = (1 - p, row)
    to_c = (p, row + 1 - 2 * c)
    to_y = (p, row + 2 - 4 * y)
    to_a = (p, row + 4 - 8 * level)
    to_b = (p, (3 - z) * 4 + y * 2 + c)
    opposite = 2 - 2 * group
    to_far = [(group, (opposite + n) * 4 + y * 2 + c) for n in (0, 1)]
    mine = level * 4 + y * 2 + c

    def tile_copy(index, slot):
        where = pl.ds(pl.multiple_of(index * TILE, 8), TILE)
        return pltpu.make_async_copy(
            force_ref.at[:, where, :], tiles.at[slot], tile_sem.at[slot]
        )

    tile_copy(0, 0).start()
    tile_copy(1, 1).start()

    own[0, 0] = start_ref[...]
    own[0, 1] = start_ref[...]
    own[1] = jnp.zeros((points, rows, 128), jnp.float32)
    centre = 0.5 * (upper_ref[0] + lower_ref[0])
    spread = 0.5 * (upper_ref[0] - lower_ref[0])
    line = lax.broadcasted_iota(jnp.int32, (8, 128), 0)
    bounds[...] = jnp.where(line < 4, centre, spread)

    def block_rows(index, piece=0, count=rows):
        return pl.ds(pl.multiple_of(index * rows + piece * depth, 8), count)

    @pl.when(owner)
    def _():
        full[0, 0, block_rows(mine), :] = start_ref[...]

    barrier = pltpu.get_barrier_semaphore()
    around = [to_x, to_c, to_y, to_a]
    around += [(q, (opposite + n) * 4 + y * 2 + c) for q in (0, 1) for n in (0, 1)]
    for target in around:
        pl.semaphore_signal(barrier, inc=1, device_id=target, device_id_type=MESH)
    pl.semaphore_wait(barrier, len(around))

    bound_copy = pltpu.make_async_remote_copy(
        src_ref=bounds, dst_ref=partner_bounds, send_sem=b_sem.at[0], recv_sem=b_sem.at[1],
        device_id=to_x, device_id_type=MESH,
    )

    def send(slot, q, index, piece, kind, target, at=None):
        view = full.at[slot, q, block_rows(index, piece, depth)]
        source = view
        if kind <= NEAR:
            source = own.at[slot, q, pl.ds(pl.multiple_of(piece * depth, 8), depth)]
        return pltpu.make_async_remote_copy(
            src_ref=source, dst_ref=view,
            send_sem=send_sem.at[q, kind, piece if at is None else at],
            recv_sem=recv_sem.at[slot, q, index, piece],
            device_id=target, device_id_type=MESH,
        )

    def index_of(flipped_level, flipped_y, flipped_c):
        zz = 1 - level if flipped_level else level
        yy = 1 - y if flipped_y else y
        cc = 1 - c if flipped_c else c
        return zz * 4 + yy * 2 + cc

    def far_sends(slot, q):
        return [send(slot, q, mine, far_piece, FAR + n, to_far[n], 0) for n in (0, 1)]

    def near_send(slot, q, piece):
        return send(slot, q, mine, piece, NEAR, to_a)

    def lane_sends(slot, q, which, piece):
        index = index_of(which == 1, False, False)
        return (
            send(slot, q, index, piece, ACROSS_Y + which, to_y),
            send(slot, q, index, piece, ACROSS_C + which, to_c),
        )

    def relay_send(slot, q, which, piece):
        return send(slot, q, index_of(which == 1, True, False), piece, RELAY_C + which, to_c)

    def await_block(slot, q, index, piece):
        send(slot, q, index, piece, ACROSS_C, to_c).wait_recv()

    def direct(slot, q, piece):
        @pl.when(far_piece == piece)
        def _():
            for copy in far_sends(slot, q):
                copy.start()

        @pl.when(owner)
        def _():
            near_send(slot, q, piece).start()
            for copy in lane_sends(slot, q, 0, piece):
                copy.start()

    def lanes(slot, q):
        for piece in range(PIECES):
            @pl.when(not_owner)
            def _():
                await_block(slot, q, index_of(False, False, False), piece)
                for copy in lane_sends(slot, q, 0, piece):
                    copy.start()

            await_block(slot, q, index_of(True, False, False), piece)
            for copy in lane_sends(slot, q, 1, piece):
                copy.start()

    def relays(slot, q):
        for piece in range(PIECES):
            for which in (0, 1):
                await_block(slot, q, index_of(which == 1, True, False), piece)
                relay_send(slot, q, which, piece).start()

    def collect(slot, q):
        for flipped_y in (False, True):
            for piece in range(PIECES):
                for which in (False, True):
                    await_block(slot, q, index_of(which, flipped_y, True), piece)

    def await_sends(slot, q):
        for copy in far_sends(slot, q):
            copy.wait_send()
        for piece in range(PIECES):
            pl.when(owner)(near_send(slot, q, piece).wait_send)
            for which in (0, 1):
                for copy in lane_sends(slot, q, which, piece):
                    copy.wait_send()
                relay_send(slot, q, which, piece).wait_send()

    def partial_copy(slot, q, piece):
        where = pl.ds(piece * depth, depth)
        return pltpu.make_async_remote_copy(
            src_ref=part.at[q, where], dst_ref=other.at[slot, q, where],
            send_sem=x_send.at[q, piece], recv_sem=x_recv.at[slot, q, piece],
            device_id=to_x, device_id_type=MESH,
        )

    def divide(slot, q):
        values = full[slot, q]
        upper = values.astype(jnp.bfloat16)
        split[:, :128] = upper
        split[:, 128:] = (values - upper.astype(jnp.float32)).astype(jnp.bfloat16)

    def multiply(q, piece):
        def stacked(ref):
            return ref[q, piece].reshape(2 * depth, cols)

        wide = jnp.dot(stacked(high), split[...], preferred_element_type=jnp.float32)
        rest = jnp.dot(stacked(low), split[:, :128], preferred_element_type=jnp.float32)
        image = wide[:, :128] + (wide[:, 128:] + rest)
        part[q, piece * depth:(piece + 1) * depth] = (
            image[:depth] + sign_row(-1.0, 1.0) * pltpu.roll(image[depth:], 64, 1)
        )

    def update(slot, q, piece, weight, keep):
        mine_q = p == q
        where = slice(piece * depth, (piece + 1) * depth)
        centre = jnp.where(mine_q, bounds[0:1, :], partner_bounds[0:1, :])
        spread = jnp.where(mine_q, bounds[4:5, :], partner_bounds[4:5, :])
        current = own[slot, q, where]
        previous = own[1 - slot, q, where]
        image = part[q, where] + other[slot, q, where]
        following = (image - centre * current) * (weight / spread) - jnp.where(keep, previous, 0.0)
        own[1 - slot, q, where] = following

        @pl.when(owner)
        def _():
            full[1 - slot, q, block_rows(mine, piece, depth), :] = following

    turns = [
        [
            sum(qpoints_ref[q, n] * offsets_ref[n, 1 + pair] for n in range(3))
            for pair in range(pairs)
        ]
        for q in range(points)
    ]
    cosines = [[eighth_cosine(turn) for turn in turns[q]] for q in range(points)]
    sines = [[eighth_cosine(turn - QDEN // 4) for turn in turns[q]] for q in range(points)]

    def assemble(tile, carry):
        slot = tile % 2
        tile_copy(tile, slot).wait()
        piece = tile * TILE // depth
        place = pl.ds(pl.multiple_of(tile * TILE - piece * depth, 16), TILE)
        width = 256
        for at in range(cols // width):
            span = slice(at * width, (at + 1) * width)
            real = [tiles[slot, 0, :, span]] * points
            imag = [None] * points
            for pair in range(pairs):
                first = tiles[slot, 1 + pair, :, span]
                second = tiles[slot, 1 + pair + pairs, :, span]
                total, difference = first + second, first - second
                for q in range(points):
                    real[q] = real[q] + cosines[q][pair] * total
                    term = sines[q][pair] * difference
                    imag[q] = term if pair == 0 else imag[q] + term
            for q in range(points):
                for which, value in ((0, real[q]), (1, imag[q])):
                    upper = value.astype(jnp.bfloat16)
                    high[q, piece, which, place, span] = upper
                    rest = (value - upper.astype(jnp.float32)).astype(jnp.bfloat16)
                    low[q, piece, which, place, span] = rest

        @pl.when(tile + 2 < rows // TILE)
        def _():
            tile_copy(tile + 2, slot).start()

        return carry

    bound_copy.start()
    for piece in range(PIECES):
        direct(0, 0, piece)
    third = rows // TILE // 3
    lax.fori_loop(0, 2 * third, assemble, 0)
    lanes(0, 0)
    lax.fori_loop(2 * third, 3 * third, assemble, 0)
    relays(0, 0)
    bound_copy.wait()

    def turn(k, q):
        slot = k % 2
        later = k > 0
        middle = k < STEPS - 1
        weight = jnp.where(slot == 0, 1.0, 2.0)

        def gather():
            if q == 1:
                lanes(slot, q)
                relays(slot, q)
            else:
                @pl.when(later)
                def _():
                    lanes(slot, q)
                    relays(slot, q)
            collect(slot, q)
            divide(slot, q)

        if q == 0:
            gather()
        else:
            pl.when(later)(gather)
        for piece in range(PIECES):
            pl.when(later)(partial_copy(1 - slot, q, piece).wait_send)
            multiply(q, piece)
            pl.when(middle)(partial_copy(slot, q, piece).start)
        if q == 0:
            await_sends(slot, q)
        else:
            pl.when(later)(functools.partial(await_sends, slot, q))

        @pl.when(middle)
        def _():
            for piece in range(PIECES):
                partial_copy(slot, q, piece).wait_recv()
                update(slot, q, piece, weight, slot == 1)
                direct(1 - slot, q, piece)

    def step(k, carry):
        turn(k, 0)
        turn(k, 1)
        return carry

    lax.fori_loop(0, STEPS, step, 0)
    slot = (STEPS - 1) % 2
    final_ref[...] = own[slot, p]

    def gram(left, right):
        whole = lax.dot_general(
            left, right, (((0,), (0,)), ((), ())), precision=highest,
            preferred_element_type=jnp.float32,
        )
        return whole[:64] + sign_row(1.0, -1.0) * pltpu.roll(whole[64:], 64, 1)

    sums[5, 0] = gram(own[slot, 1 - p], part[1 - p])
    cross = pltpu.make_async_remote_copy(
        src_ref=sums.at[5, 0], dst_ref=arrived.at[4, 0], send_sem=g_send.at[4],
        recv_sem=g_recv.at[4], device_id=to_x, device_id_type=MESH,
    )
    cross.start()
    sums[0, 0] = gram(own[slot, p], own[slot, p])
    own_projected = gram(own[slot, p], part[p])
    cross.wait()
    sums[0, 1] = own_projected + arrived[4, 0]
    for stage, target in enumerate((to_c, to_y, to_a, to_b)):
        copy = pltpu.make_async_remote_copy(
            src_ref=sums.at[stage], dst_ref=arrived.at[stage], send_sem=g_send.at[stage],
            recv_sem=g_recv.at[stage], device_id=target, device_id_type=MESH,
        )
        copy.start()
        copy.wait()
        sums[stage + 1] = sums[stage] + arrived[stage]
    gram_ref[...] = sums[4]


def filtered(offsets, qpoints, lower_bound, upper_bound, force_constants, start_vectors):
    cells, rows, cols = force_constants.shape
    points = qpoints.shape[0]
    vmem = pl.BlockSpec(memory_space=pltpu.VMEM)
    smem = pl.BlockSpec(memory_space=pltpu.SMEM)
    dma = pltpu.SemaphoreType.DMA
    single = jnp.float32
    matrix = pltpu.VMEM((points, PIECES, 2, rows // PIECES, cols), jnp.bfloat16)
    return pl.pallas_call(
        filter_kernel,
        out_shape=(
            jax.ShapeDtypeStruct((rows, 128), single),
            jax.ShapeDtypeStruct((2, 64, 128), single),
        ),
        in_specs=[smem] * 4 + [pl.BlockSpec(memory_space=pl.ANY), vmem],
        out_specs=(vmem, vmem),
        scratch_shapes=[
            pltpu.VMEM((2, cells, TILE, cols), single),
            matrix,
            matrix,
            pltpu.VMEM((2, points, cols, 128), single),
            pltpu.VMEM((2, points, rows, 128), single),
            pltpu.VMEM((points, rows, 128), single),
            pltpu.VMEM((2, points, rows, 128), single),
            pltpu.VMEM((cols, 256), jnp.bfloat16),
            pltpu.VMEM((8, 128), single),
            pltpu.VMEM((8, 128), single),
            pltpu.VMEM((6, 2, 64, 128), single),
            pltpu.VMEM((5, 2, 64, 128), single),
            dma((2,)),
            dma((points, KINDS, PIECES)),
            dma((2, points, 8, PIECES)),
            dma((points, PIECES)),
            dma((2, points, PIECES)),
            dma((2,)),
            dma((5,)),
            dma((5,)),
        ],
        compiler_params=pltpu.CompilerParams(
            collective_id=0, has_side_effects=True, vmem_limit_bytes=56 * 1024 * 1024
        ),
    )(offsets.T, qpoints, lower_bound, upper_bound, force_constants, start_vectors)


def finish_kernel(scale, final_ref, gram_ref, basis_ref, ritz_ref):
    size = gram_ref.shape[1]
    tile = 8
    gram = [gram_ref[0, t * tile:(t + 1) * tile, :] for t in range(size // tile)]
    lane = lax.broadcasted_iota(jnp.int32, (tile, 128), 1)
    line = lax.broadcasted_iota(jnp.int32, (tile, 128), 0)
    inverse = [jnp.where(lane == line + t * tile, 1.0, 0.0) for t in range(size // tile)]
    turn = sign_row(-1.0, 1.0)
    for j in range(size):
        home, at = j // tile, j % tile
        row = gram[home][at:at + 1, :]
        pivot = row[:, j:j + 1]
        row = row / pivot
        mate = inverse[home][at:at + 1, :] / pivot
        row_turned = turn * pltpu.roll(row, 64, 1)
        mate_turned = turn * pltpu.roll(mate, 64, 1)
        for t in range(home, size // tile):
            real = gram[t][:, j:j + 1]
            imag = gram[t][:, 64 + j:65 + j]
            if t == home:
                below = line[:, :1] > at
                real = jnp.where(below, real, 0.0)
                imag = jnp.where(below, imag, 0.0)
            gram[t] = gram[t] - (real * row + imag * row_turned)
            inverse[t] = inverse[t] - (real * mate + imag * mate_turned)
    scaled = []
    for t in range(size // tile):
        diagonal = jnp.sum(jnp.where(lane == line + t * tile, gram[t], 0.0), axis=1, keepdims=True)
        scaled.append(inverse[t] / jnp.sqrt(diagonal))
    whole = jnp.concatenate(scaled, axis=0)
    paired = jnp.concatenate([whole, turn * pltpu.roll(whole, 64, 1)], axis=0)

    def against(left):
        return lax.dot_general(
            left, paired, (((1,), (1,)), ((), ())), precision=highest,
            preferred_element_type=jnp.float32,
        )

    basis_ref[...] = scale * against(final_ref[...])
    half = against(gram_ref[1])
    ritz_ref[...] = product(whole, jnp.concatenate([half, turn * pltpu.roll(half, 64, 1)], axis=0))


def finish(final_pass, grams, modes):
    vmem = pl.BlockSpec(memory_space=pltpu.VMEM)
    return pl.pallas_call(
        functools.partial(finish_kernel, math.sqrt(modes)),
        out_shape=(
            jax.ShapeDtypeStruct(final_pass.shape, jnp.float32),
            jax.ShapeDtypeStruct(grams.shape[1:], jnp.float32),
        ),
        in_specs=[vmem] * 2,
        out_specs=(vmem, vmem),
    )(final_pass, grams)


def on_block(force_constants, offsets, qpoints, lower_bound, upper_bound, start_vectors):
    final_pass, grams = filtered(
        offsets, qpoints, lower_bound, upper_bound, force_constants, start_vectors
    )
    basis_local, ritz_local = finish(final_pass, grams, MODES)
    return (basis_local[None], ritz_local[None])


def solution(mesh):
    paired = mesh.shape["pb"] == 2 and mesh.shape["row"] == 16
    return jax.shard_map(
        on_block if paired else on_device,
        mesh=mesh,
        in_specs=(P(None, "row", "pb"), P(), P(), P("pb"), P("pb"), P("row", None)),
        out_specs=(P("pb", "row", None), P("pb", None, None)),
        check_vma=False,
    )
```

time: 180 us -> 177 us (0.983)
  local copies, waits for them, and re-layouts: 2.01 us -> 0 us
    pallas_call x1 -> x0, Pallas kernels: 14.3 us -> none  [assemble(): pl.pallas_call(assemble_kernel, grid=(rows // tile,), out_shape=(shape, s...]
    pallas_call x1, Pallas kernels: 148 us -> 162 us  [filtered(): pl.pallas_call(filter_kernel, out_shape=(jax.ShapeDtypeStruct((rows, 128)...]
where the time goes in v1:
time: 177 us; the launch traced here: 176 us
  Pallas kernels  175 us (99%)
  between operations  1.93 us (1%)
    pallas_call x1, Pallas kernels, filtered(): pl.pallas_call(filter_kernel, out_shape=(jax.ShapeDtypeStruct((rows, 128)...  162 us
    pallas_call x1, Pallas kernels, finish(): pl.pallas_call(functools.partial(finish_kernel, math.sqrt(modes)), out_sh...  12.1 us

profile of v1, /device:TPU:0, one launch (start us, length us, event | category | flops | bytes accessed | tf_op | source)
XLA Modules:
  0.0 176.5 jit_solution(7956736209067087196)
XLA Ops:
  1.9 162.5 %shard_map.77 = (f32[288,128]{1,0:T(8,128)}, f32[2,64,128]{2,1,0:T(8,128)}) custom-call(s32[3,9]{1,0:T(4,128)} %bitcast.3, s32[2,3]{1,0:T(2,128)} %qpoints_ref.1, f32[1]{0:T(128)S(6)} %copy.8.lower_ref, f32[1]{0:T(128)S(6)} %copy.9.upper_ref, f32[9,288,2304]{2,1,0:T(8,128)} %force_ref.1, f32[288,128]{1,0:T(8,128)} %start_ref.1), custom_call_target="tpu_custom_call" | custom-call | tf_op jit(solution)/shard_map/pallas_call | solution.py:469
  164.4 12.1 %shard_map.78 = (f32[288,128]{1,0:T(8,128)}, f32[64,128]{1,0:T(8,128)}) custom-call(f32[288,128]{1,0:T(8,128)} %get-tuple-element.6.final_ref, f32[2,64,128]{2,1,0:T(8,128)} %get-tuple-element.7.gram_ref), custom_call_target="tpu_custom_call" | custom-call | tf_op jit(solution)/shard_map/pallas_call | solution.py:550

commit v2 on v1

--- a/solution.py
+++ b/solution.py
@@ -125,9 +125,11 @@
 
 STEPS = 5
 PIECES = 2
+SUBS = 3
+AHEAD = ((0,), (1,), (2,))
 TILE = 48
-FAR, NEAR, ACROSS_Y, ACROSS_C, RELAY_C = 0, 2, 3, 5, 7
-KINDS = 9
+FAR, NEAR, ACROSS_Y, ACROSS_C = 0, 1, 2, 3
+KINDS = 4
 MESH = pl.DeviceIdType.MESH
 
 
@@ -148,7 +150,7 @@
 def filter_kernel(
     offsets_ref, qpoints_ref, lower_ref, upper_ref, force_ref, start_ref, final_ref, gram_ref,
     tiles, high, low, full, own, part, other, split, bounds, partner_bounds, sums, arrived,
-    tile_sem, send_sem, recv_sem, x_send, x_recv, b_sem, g_send, g_recv,
+    tile_sem, send_sem, level_recv, lane_recv, core_recv, x_send, x_recv, b_sem, g_send, g_recv,
 ):
     p = lax.axis_index("pb")
     row = lax.axis_index("row")
@@ -171,7 +173,12 @@
     to_b = (p, (3 - z) * 4 + y * 2 + c)
     opposite = 2 - 2 * group
     to_far = [(group, (opposite + n) * 4 + y * 2 + c) for n in (0, 1)]
-    mine = level * 4 + y * 2 + c
+
+    def guarded(condition, action):
+        if condition is None:
+            action()
+        else:
+            pl.when(condition)(action)
 
     def tile_copy(index, slot):
         where = pl.ds(pl.multiple_of(index * TILE, 8), TILE)
@@ -190,12 +197,17 @@
     line = lax.broadcasted_iota(jnp.int32, (8, 128), 0)
     bounds[...] = jnp.where(line < 4, centre, spread)
 
-    def block_rows(index, piece=0, count=rows):
-        return pl.ds(pl.multiple_of(index * rows + piece * depth, 8), count)
+    def piece_rows(piece):
+        return pl.ds(pl.multiple_of(piece * depth, 8), depth)
+
+    grain = depth // SUBS
+
+    def sub_rows(piece, sub):
+        return pl.ds(pl.multiple_of(piece * depth + sub * grain, 8), grain)
 
     @pl.when(owner)
     def _():
-        full[0, 0, block_rows(mine), :] = start_ref[...]
+        full[0, 0, level, y, c] = start_ref[...]
 
     barrier = pltpu.get_barrier_semaphore()
     around = [to_x, to_c, to_y, to_a]
@@ -209,91 +221,75 @@
         device_id=to_x, device_id_type=MESH,
     )
 
-    def send(slot, q, index, piece, kind, target, at=None):
-        view = full.at[slot, q, block_rows(index, piece, depth)]
-        source = view
-        if kind <= NEAR:
-            source = own.at[slot, q, pl.ds(pl.multiple_of(piece * depth, 8), depth)]
+    def send(source, view, q, kind, arrival, target):
         return pltpu.make_async_remote_copy(
-            src_ref=source, dst_ref=view,
-            send_sem=send_sem.at[q, kind, piece if at is None else at],
-            recv_sem=recv_sem.at[slot, q, index, piece],
+            src_ref=source, dst_ref=view, send_sem=send_sem.at[q, kind], recv_sem=arrival,
             device_id=target, device_id_type=MESH,
         )
 
-    def index_of(flipped_level, flipped_y, flipped_c):
-        zz = 1 - level if flipped_level else level
-        yy = 1 - y if flipped_y else y
-        cc = 1 - c if flipped_c else c
-        return zz * 4 + yy * 2 + cc
-
-    def far_sends(slot, q):
-        return [send(slot, q, mine, far_piece, FAR + n, to_far[n], 0) for n in (0, 1)]
-
-    def near_send(slot, q, piece):
-        return send(slot, q, mine, piece, NEAR, to_a)
-
-    def lane_sends(slot, q, which, piece):
-        index = index_of(which == 1, False, False)
-        return (
-            send(slot, q, index, piece, ACROSS_Y + which, to_y),
-            send(slot, q, index, piece, ACROSS_C + which, to_c),
-        )
-
-    def relay_send(slot, q, which, piece):
-        return send(slot, q, index_of(which == 1, True, False), piece, RELAY_C + which, to_c)
-
-    def await_block(slot, q, index, piece):
-        send(slot, q, index, piece, ACROSS_C, to_c).wait_recv()
+    def level_copy(slot, q, at_level, piece, sub, kind, target):
+        where = sub_rows(piece, sub)
+        return send(
+            own.at[slot, q, where], full.at[slot, q, at_level, y, c, where], q, kind,
+            level_recv.at[slot, q, at_level, piece, sub], target,
+        )
+
+    def lane_copy(slot, q, yy, piece, sub):
+        view = full.at[slot, q, :, yy, c, sub_rows(piece, sub)]
+        return send(view, view, q, ACROSS_Y, lane_recv.at[slot, q, piece, sub], to_y)
+
+    def core_copy(slot, q, view):
+        return send(view, view, q, ACROSS_C, core_recv.at[slot, q], to_c)
 
     def direct(slot, q, piece):
         @pl.when(far_piece == piece)
         def _():
-            for copy in far_sends(slot, q):
-                copy.start()
-
+            for sub in range(SUBS):
+                for target in to_far:
+                    level_copy(slot, q, level, piece, sub, FAR, target).start()
+
+    def near(slot, q):
         @pl.when(owner)
         def _():
-            near_send(slot, q, piece).start()
-            for copy in lane_sends(slot, q, 0, piece):
-                copy.start()
-
-    def lanes(slot, q):
+            for sub in range(SUBS):
+                for piece in range(PIECES):
+                    level_copy(slot, q, level, piece, sub, NEAR, to_a).start()
+
+    def lanes(slot, q, sub):
         for piece in range(PIECES):
             @pl.when(not_owner)
             def _():
-                await_block(slot, q, index_of(False, False, False), piece)
-                for copy in lane_sends(slot, q, 0, piece):
-                    copy.start()
-
-            await_block(slot, q, index_of(True, False, False), piece)
-            for copy in lane_sends(slot, q, 1, piece):
-                copy.start()
+                level_copy(slot, q, level, piece, sub, NEAR, to_a).wait_recv()
+
+            level_copy(slot, q, 1 - level, piece, sub, NEAR, to_a).wait_recv()
+            lane_copy(slot, q, y, piece, sub).start()
+        if sub == SUBS - 1:
+            core_copy(slot, q, full.at[slot, q, :, y, c]).start()
 
     def relays(slot, q):
-        for piece in range(PIECES):
-            for which in (0, 1):
-                await_block(slot, q, index_of(which == 1, True, False), piece)
-                relay_send(slot, q, which, piece).start()
+        for sub in range(SUBS):
+            for piece in range(PIECES):
+                lane_copy(slot, q, 1 - y, piece, sub).wait_recv()
+                core_copy(slot, q, full.at[slot, q, :, 1 - y, c, sub_rows(piece, sub)]).start()
 
     def collect(slot, q):
-        for flipped_y in (False, True):
-            for piece in range(PIECES):
-                for which in (False, True):
-                    await_block(slot, q, index_of(which, flipped_y, True), piece)
+        core_copy(slot, q, full.at[slot, q, :, :, 1 - c]).wait_recv()
 
     def await_sends(slot, q):
-        for copy in far_sends(slot, q):
-            copy.wait_send()
-        for piece in range(PIECES):
-            pl.when(owner)(near_send(slot, q, piece).wait_send)
-            for which in (0, 1):
-                for copy in lane_sends(slot, q, which, piece):
-                    copy.wait_send()
-                relay_send(slot, q, which, piece).wait_send()
+        block = own.at[slot, q]
+        send(block, block, q, FAR, core_recv.at[slot, q], to_c).wait_send()
+
+        @pl.when(owner)
+        def _():
+            send(block, block, q, NEAR, core_recv.at[slot, q], to_c).wait_send()
+
+        lane = full.at[slot, q, :, y, c]
+        send(lane, lane, q, ACROSS_Y, core_recv.at[slot, q], to_c).wait_send()
+        half = full.at[slot, q, :, :, c]
+        core_copy(slot, q, half).wait_send()
 
     def partial_copy(slot, q, piece):
-        where = pl.ds(piece * depth, depth)
+        where = pl.ds(pl.multiple_of(piece * depth, 8), depth)
         return pltpu.make_async_remote_copy(
             src_ref=part.at[q, where], dst_ref=other.at[slot, q, where],
             send_sem=x_send.at[q, piece], recv_sem=x_recv.at[slot, q, piece],
@@ -301,7 +297,7 @@
         )
 
     def divide(slot, q):
-        values = full[slot, q]
+        values = full[slot, q].reshape(cols, 128)
         upper = values.astype(jnp.bfloat16)
         split[:, :128] = upper
         split[:, 128:] = (values - upper.astype(jnp.float32)).astype(jnp.bfloat16)
@@ -313,13 +309,13 @@
         wide = jnp.dot(stacked(high), split[...], preferred_element_type=jnp.float32)
         rest = jnp.dot(stacked(low), split[:, :128], preferred_element_type=jnp.float32)
         image = wide[:, :128] + (wide[:, 128:] + rest)
-        part[q, piece * depth:(piece + 1) * depth] = (
+        part[q, pl.ds(pl.multiple_of(piece * depth, 8), depth)] = (
             image[:depth] + sign_row(-1.0, 1.0) * pltpu.roll(image[depth:], 64, 1)
         )
 
     def update(slot, q, piece, weight, keep):
         mine_q = p == q
-        where = slice(piece * depth, (piece + 1) * depth)
+        where = pl.ds(pl.multiple_of(piece * depth, 8), depth)
         centre = jnp.where(mine_q, bounds[0:1, :], partner_bounds[0:1, :])
         spread = jnp.where(mine_q, bounds[4:5, :], partner_bounds[4:5, :])
         current = own[slot, q, where]
@@ -330,7 +326,7 @@
 
         @pl.when(owner)
         def _():
-            full[1 - slot, q, block_rows(mine, piece, depth), :] = following
+            full[1 - slot, q, level, y, c, where] = following
 
     turns = [
         [
@@ -376,54 +372,54 @@
     bound_copy.start()
     for piece in range(PIECES):
         direct(0, 0, piece)
+    near(0, 0)
     third = rows // TILE // 3
     lax.fori_loop(0, 2 * third, assemble, 0)
-    lanes(0, 0)
+    for sub in range(SUBS):
+        lanes(0, 0, sub)
     lax.fori_loop(2 * third, 3 * third, assemble, 0)
-    relays(0, 0)
     bound_copy.wait()
 
-    def turn(k, q):
+    def apply_matrix(k, q):
         slot = k % 2
         later = k > 0
         middle = k < STEPS - 1
-        weight = jnp.where(slot == 0, 1.0, 2.0)
-
-        def gather():
-            if q == 1:
-                lanes(slot, q)
-                relays(slot, q)
-            else:
-                @pl.when(later)
-                def _():
-                    lanes(slot, q)
-                    relays(slot, q)
+        other_slot, ready = (slot, later) if q == 0 else (1 - slot, middle)
+
+        def ahead(stage):
+            for sub in AHEAD[stage]:
+                pl.when(ready)(functools.partial(lanes, other_slot, 1 - q, sub))
+
+        def finish_gather():
+            relays(slot, q)
+
+        def finish_collect():
             collect(slot, q)
             divide(slot, q)
 
-        if q == 0:
-            gather()
-        else:
-            pl.when(later)(gather)
-        for piece in range(PIECES):
+        guarded(None if q == 0 else later, finish_gather)
+        ahead(0)
+        guarded(None if q == 0 else later, finish_collect)
+        for stage, piece in enumerate((1 - far_piece, far_piece)):
             pl.when(later)(partial_copy(1 - slot, q, piece).wait_send)
             multiply(q, piece)
             pl.when(middle)(partial_copy(slot, q, piece).start)
-        if q == 0:
-            await_sends(slot, q)
-        else:
-            pl.when(later)(functools.partial(await_sends, slot, q))
-
-        @pl.when(middle)
-        def _():
-            for piece in range(PIECES):
-                partial_copy(slot, q, piece).wait_recv()
-                update(slot, q, piece, weight, slot == 1)
-                direct(1 - slot, q, piece)
+            ahead(1 + stage)
+        guarded(None if q == 0 else later, functools.partial(await_sends, slot, q))
+
+    def advance(k, q):
+        slot = k % 2
+        weight = jnp.where(slot == 0, 1.0, 2.0)
+        for piece in (far_piece, 1 - far_piece):
+            partial_copy(slot, q, piece).wait_recv()
+            update(slot, q, piece, weight, slot == 1)
+            direct(1 - slot, q, piece)
+        near(1 - slot, q)
 
     def step(k, carry):
-        turn(k, 0)
-        turn(k, 1)
+        for q in (0, 1):
+            apply_matrix(k, q)
+            pl.when(k < STEPS - 1)(functools.partial(advance, k, q))
         return carry
 
     lax.fori_loop(0, STEPS, step, 0)
@@ -478,7 +474,7 @@
             pltpu.VMEM((2, cells, TILE, cols), single),
             matrix,
             matrix,
-            pltpu.VMEM((2, points, cols, 128), single),
+            pltpu.VMEM((2, points, 2, 2, 2, rows, 128), single),
             pltpu.VMEM((2, points, rows, 128), single),
             pltpu.VMEM((points, rows, 128), single),
             pltpu.VMEM((2, points, rows, 128), single),
@@ -488,8 +484,10 @@
             pltpu.VMEM((6, 2, 64, 128), single),
             pltpu.VMEM((5, 2, 64, 128), single),
             dma((2,)),
-            dma((points, KINDS, PIECES)),
-            dma((2, points, 8, PIECES)),
+            dma((points, KINDS)),
+            dma((2, points, 2, PIECES, SUBS)),
+            dma((2, points, PIECES, SUBS)),
+            dma((2, points)),
             dma((points, PIECES)),
             dma((2, points, PIECES)),
             dma((2,)),

time: 177 us -> 141 us (0.80)
  Pallas kernels: 175 us -> 139 us
    pallas_call x1, Pallas kernels: 162 us -> 127 us  [filtered(): pl.pallas_call(filter_kernel, out_shape=(jax.ShapeDtypeStruct((rows, 128)...]
where the time goes in v2:
time: 141 us
  Pallas kernels  139 us (99%)
  between operations  1.93 us (1%)
    pallas_call x1, Pallas kernels, filtered(): pl.pallas_call(filter_kernel, out_shape=(jax.ShapeDtypeStruct((rows, 128)...  127 us
    pallas_call x1, Pallas kernels, finish(): pl.pallas_call(functools.partial(finish_kernel, math.sqrt(modes)), out_sh...  12.1 us

profile of v2, /device:TPU:0, one launch (start us, length us, event | category | flops | bytes accessed | tf_op | source)
XLA Modules:
  0.0 140.7 jit_solution(14204115179667680495)
XLA Ops:
  1.9 126.7 %shard_map.77 = (f32[288,128]{1,0:T(8,128)}, f32[2,64,128]{2,1,0:T(8,128)}) custom-call(s32[3,9]{1,0:T(4,128)} %bitcast.3, s32[2,3]{1,0:T(2,128)} %qpoints_ref.1, f32[1]{0:T(128)S(6)} %copy.8.lower_ref, f32[1]{0:T(128)S(6)} %copy.9.upper_ref, f32[9,288,2304]{2,1,0:T(8,128)} %force_ref.1, f32[288,128]{1,0:T(8,128)} %start_ref.1), custom_call_target="tpu_custom_call" | custom-call | tf_op jit(solution)/shard_map/pallas_call | solution.py:465
  128.6 12.1 %shard_map.78 = (f32[288,128]{1,0:T(8,128)}, f32[64,128]{1,0:T(8,128)}) custom-call(f32[288,128]{1,0:T(8,128)} %get-tuple-element.6.final_ref, f32[2,64,128]{2,1,0:T(8,128)} %get-tuple-element.7.gram_ref), custom_call_target="tpu_custom_call" | custom-call | tf_op jit(solution)/shard_map/pallas_call | solution.py:548

commit v3 on v2

--- a/solution.py
+++ b/solution.py
@@ -128,6 +128,7 @@
 SUBS = 3
 AHEAD = ((0,), (1,), (2,))
 TILE = 48
+GROUP = 3
 FAR, NEAR, ACROSS_Y, ACROSS_C = 0, 1, 2, 3
 KINDS = 4
 MESH = pl.DeviceIdType.MESH
@@ -147,9 +148,41 @@
     return value
 
 
+def turned(values):
+    return sign_row(-1.0, 1.0) * pltpu.roll(values, 64, 1)
+
+
+def eliminate(factor, start, stop):
+    size = factor.shape[1]
+    tile = 8
+    line = lax.broadcasted_iota(jnp.int32, (tile, 1), 0)
+    first = start // tile
+    pieces = [slice(t * tile, (t + 1) * tile) for t in range(size // tile)]
+    gram = {t: factor[0, pieces[t]] for t in range(first, size // tile)}
+    inverse = {t: factor[1, pieces[t]] for t in range(first, size // tile)}
+    for j in range(start, stop):
+        home, at = j // tile, j % tile
+        row = gram[home][at:at + 1, :]
+        mate = inverse[home][at:at + 1, :]
+        row_turned, mate_turned = turned(row), turned(mate)
+        scale = 1.0 / row[:, j:j + 1]
+        for t in range(home, size // tile):
+            real = gram[t][:, j:j + 1] * scale
+            imag = gram[t][:, size + j:size + j + 1] * scale
+            if t == home:
+                real = jnp.where(line > at, real, 0.0)
+                imag = jnp.where(line > at, imag, 0.0)
+            gram[t] = gram[t] - (real * row + imag * row_turned)
+            inverse[t] = inverse[t] - (real * mate + imag * mate_turned)
+    for t in gram:
+        factor[0, pieces[t]] = gram[t]
+        factor[1, pieces[t]] = inverse[t]
+
+
 def filter_kernel(
-    offsets_ref, qpoints_ref, lower_ref, upper_ref, force_ref, start_ref, final_ref, gram_ref,
-    tiles, high, low, full, own, part, other, split, bounds, partner_bounds, sums, arrived,
+    scale,
+    offsets_ref, qpoints_ref, lower_ref, upper_ref, force_ref, start_ref, basis_ref, ritz_ref,
+    tiles, high, low, full, own, part, other, split, bounds, partner_bounds, sums, arrived, factor,
     tile_sem, send_sem, level_recv, lane_recv, core_recv, x_send, x_recv, b_sem, g_send, g_recv,
 ):
     p = lax.axis_index("pb")
@@ -172,12 +205,15 @@
     to_a = (p, row + 4 - 8 * level)
     to_b = (p, (3 - z) * 4 + y * 2 + c)
     opposite = 2 - 2 * group
+    to_xc = (1 - p, row + 1 - 2 * c)
+    to_ay = (p, row + 4 - 8 * level + 2 - 4 * y)
+    to_z = (p, (opposite + level) * 4 + y * 2 + c)
     to_far = [(group, (opposite + n) * 4 + y * 2 + c) for n in (0, 1)]
 
     def guarded(condition, action):
-        if condition is None:
+        if condition is True:
             action()
-        else:
+        elif condition is not False:
             pl.when(condition)(action)
 
     def tile_copy(index, slot):
@@ -185,6 +221,12 @@
         return pltpu.make_async_copy(
             force_ref.at[:, where, :], tiles.at[slot], tile_sem.at[slot]
         )
+
+    barrier = pltpu.get_barrier_semaphore()
+    around = [to_x, to_c, to_y, to_a, to_xc, to_ay]
+    around += [(q, (opposite + n) * 4 + y * 2 + c) for q in (0, 1) for n in (0, 1)]
+    for target in around:
+        pl.semaphore_signal(barrier, inc=1, device_id=target, device_id_type=MESH)
 
     tile_copy(0, 0).start()
     tile_copy(1, 1).start()
@@ -209,11 +251,6 @@
     def _():
         full[0, 0, level, y, c] = start_ref[...]
 
-    barrier = pltpu.get_barrier_semaphore()
-    around = [to_x, to_c, to_y, to_a]
-    around += [(q, (opposite + n) * 4 + y * 2 + c) for q in (0, 1) for n in (0, 1)]
-    for target in around:
-        pl.semaphore_signal(barrier, inc=1, device_id=target, device_id_type=MESH)
     pl.semaphore_wait(barrier, len(around))
 
     bound_copy = pltpu.make_async_remote_copy(
@@ -241,10 +278,15 @@
     def core_copy(slot, q, view):
         return send(view, view, q, ACROSS_C, core_recv.at[slot, q], to_c)
 
-    def direct(slot, q, piece):
+    def tiles_of(piece):
+        return [piece * (depth // TILE) + n for n in range(0, depth // TILE, GROUP)]
+
+    def direct(slot, q, piece, group_at):
+        count = SUBS * GROUP * TILE // depth
+
         @pl.when(far_piece == piece)
         def _():
-            for sub in range(SUBS):
+            for sub in range(group_at * count, (group_at + 1) * count):
                 for target in to_far:
                     level_copy(slot, q, level, piece, sub, FAR, target).start()
 
@@ -288,11 +330,14 @@
         half = full.at[slot, q, :, :, c]
         core_copy(slot, q, half).wait_send()
 
-    def partial_copy(slot, q, piece):
-        where = pl.ds(pl.multiple_of(piece * depth, 8), depth)
+    def tile_rows(tile):
+        return pl.ds(pl.multiple_of(tile * TILE, 8), GROUP * TILE)
+
+    def partial_copy(slot, q, tile):
+        where = tile_rows(tile)
         return pltpu.make_async_remote_copy(
             src_ref=part.at[q, where], dst_ref=other.at[slot, q, where],
-            send_sem=x_send.at[q, piece], recv_sem=x_recv.at[slot, q, piece],
+            send_sem=x_send.at[q, tile], recv_sem=x_recv.at[slot, q, tile],
             device_id=to_x, device_id_type=MESH,
         )
 
@@ -302,20 +347,19 @@
         split[:, :128] = upper
         split[:, 128:] = (values - upper.astype(jnp.float32)).astype(jnp.bfloat16)
 
-    def multiply(q, piece):
+    def multiply(q, tile):
         def stacked(ref):
-            return ref[q, piece].reshape(2 * depth, cols)
+            return ref[q, pl.ds(tile, GROUP)].reshape(GROUP * 2 * TILE, cols)
 
         wide = jnp.dot(stacked(high), split[...], preferred_element_type=jnp.float32)
         rest = jnp.dot(stacked(low), split[:, :128], preferred_element_type=jnp.float32)
-        image = wide[:, :128] + (wide[:, 128:] + rest)
-        part[q, pl.ds(pl.multiple_of(piece * depth, 8), depth)] = (
-            image[:depth] + sign_row(-1.0, 1.0) * pltpu.roll(image[depth:], 64, 1)
-        )
-
-    def update(slot, q, piece, weight, keep):
+        image = (wide[:, :128] + (wide[:, 128:] + rest)).reshape(GROUP, 2, TILE, 128)
+        crossed = turned(image[:, 1].reshape(GROUP * TILE, 128))
+        part[q, tile_rows(tile)] = image[:, 0].reshape(GROUP * TILE, 128) + crossed
+
+    def update(slot, q, tile, weight, keep):
         mine_q = p == q
-        where = pl.ds(pl.multiple_of(piece * depth, 8), depth)
+        where = tile_rows(tile)
         centre = jnp.where(mine_q, bounds[0:1, :], partner_bounds[0:1, :])
         spread = jnp.where(mine_q, bounds[4:5, :], partner_bounds[4:5, :])
         current = own[slot, q, where]
@@ -341,27 +385,29 @@
     def assemble(tile, carry):
         slot = tile % 2
         tile_copy(tile, slot).wait()
-        piece = tile * TILE // depth
-        place = pl.ds(pl.multiple_of(tile * TILE - piece * depth, 16), TILE)
         width = 256
-        for at in range(cols // width):
-            span = slice(at * width, (at + 1) * width)
-            real = [tiles[slot, 0, :, span]] * points
+        lines = 16
+        for at in range(TILE // lines * (cols // width)):
+            start = at % (cols // width) * width
+            span = slice(start, start + width)
+            top = at // (cols // width) * lines
+            real = [tiles[slot, 0, top:top + lines, span]] * points
             imag = [None] * points
             for pair in range(pairs):
-                first = tiles[slot, 1 + pair, :, span]
-                second = tiles[slot, 1 + pair + pairs, :, span]
+                first = tiles[slot, 1 + pair, top:top + lines, span]
+                second = tiles[slot, 1 + pair + pairs, top:top + lines, span]
                 total, difference = first + second, first - second
                 for q in range(points):
                     real[q] = real[q] + cosines[q][pair] * total
                     term = sines[q][pair] * difference
                     imag[q] = term if pair == 0 else imag[q] + term
+            place = slice(top, top + lines)
             for q in range(points):
                 for which, value in ((0, real[q]), (1, imag[q])):
                     upper = value.astype(jnp.bfloat16)
-                    high[q, piece, which, place, span] = upper
+                    high[q, tile, which, place, span] = upper
                     rest = (value - upper.astype(jnp.float32)).astype(jnp.bfloat16)
-                    low[q, piece, which, place, span] = rest
+                    low[q, tile, which, place, span] = rest
 
         @pl.when(tile + 2 < rows // TILE)
         def _():
@@ -371,7 +417,8 @@
 
     bound_copy.start()
     for piece in range(PIECES):
-        direct(0, 0, piece)
+        for sub in range(depth // TILE // GROUP):
+            direct(0, 0, piece, sub)
     near(0, 0)
     third = rows // TILE // 3
     lax.fori_loop(0, 2 * third, assemble, 0)
@@ -380,51 +427,46 @@
     lax.fori_loop(2 * third, 3 * third, assemble, 0)
     bound_copy.wait()
 
-    def apply_matrix(k, q):
+    def apply_matrix(k, q, later, middle, extra=lambda stage: None):
         slot = k % 2
-        later = k > 0
-        middle = k < STEPS - 1
+        wanted = True if q == 0 else later
         other_slot, ready = (slot, later) if q == 0 else (1 - slot, middle)
 
         def ahead(stage):
             for sub in AHEAD[stage]:
-                pl.when(ready)(functools.partial(lanes, other_slot, 1 - q, sub))
-
-        def finish_gather():
-            relays(slot, q)
-
-        def finish_collect():
+                guarded(ready, functools.partial(lanes, other_slot, 1 - q, sub))
+            extra(stage)
+
+        def take():
             collect(slot, q)
             divide(slot, q)
 
-        guarded(None if q == 0 else later, finish_gather)
+        guarded(wanted, functools.partial(relays, slot, q))
         ahead(0)
-        guarded(None if q == 0 else later, finish_collect)
+        guarded(wanted, take)
         for stage, piece in enumerate((1 - far_piece, far_piece)):
-            pl.when(later)(partial_copy(1 - slot, q, piece).wait_send)
-            multiply(q, piece)
-            pl.when(middle)(partial_copy(slot, q, piece).start)
+            for tile in tiles_of(piece):
+                guarded(later, partial_copy(1 - slot, q, tile).wait_send)
+                multiply(q, tile)
+                guarded(middle, partial_copy(slot, q, tile).start)
             ahead(1 + stage)
-        guarded(None if q == 0 else later, functools.partial(await_sends, slot, q))
+        guarded(wanted, functools.partial(await_sends, slot, q))
 
     def advance(k, q):
         slot = k % 2
         weight = jnp.where(slot == 0, 1.0, 2.0)
         for piece in (far_piece, 1 - far_piece):
-            partial_copy(slot, q, piece).wait_recv()
-            update(slot, q, piece, weight, slot == 1)
-            direct(1 - slot, q, piece)
+            for sub, tile in enumerate(tiles_of(piece)):
+                partial_copy(slot, q, tile).wait_recv()
+                update(slot, q, tile, weight, slot == 1)
+                direct(1 - slot, q, piece, sub)
         near(1 - slot, q)
 
     def step(k, carry):
         for q in (0, 1):
-            apply_matrix(k, q)
-            pl.when(k < STEPS - 1)(functools.partial(advance, k, q))
+            apply_matrix(k, q, k > 0, True)
+            advance(k, q)
         return carry
-
-    lax.fori_loop(0, STEPS, step, 0)
-    slot = (STEPS - 1) % 2
-    final_ref[...] = own[slot, p]
 
     def gram(left, right):
         whole = lax.dot_general(
@@ -433,25 +475,84 @@
         )
         return whole[:64] + sign_row(1.0, -1.0) * pltpu.roll(whole[64:], 64, 1)
 
-    sums[5, 0] = gram(own[slot, 1 - p], part[1 - p])
-    cross = pltpu.make_async_remote_copy(
-        src_ref=sums.at[5, 0], dst_ref=arrived.at[4, 0], send_sem=g_send.at[4],
-        recv_sem=g_recv.at[4], device_id=to_x, device_id_type=MESH,
-    )
-    cross.start()
+    def sum_copy(kind, source, at, target):
+        return pltpu.make_async_remote_copy(
+            src_ref=sums.at[kind, source], dst_ref=arrived.at[kind, at],
+            send_sem=g_send.at[kind, at], recv_sem=g_recv.at[kind, at],
+            device_id=target, device_id_type=MESH,
+        )
+
+    def overlap_copy(stage):
+        return sum_copy(0, stage, stage, (to_c, to_y, to_a, to_b)[stage])
+
+    def add_overlap(stage):
+        overlap_copy(stage).wait()
+        sums[0, stage + 1] = sums[0, stage] + arrived[0, stage]
+        if stage < 3:
+            overlap_copy(stage + 1).start()
+
+    def projected_copies(stage):
+        plan = (
+            ((0, 0, to_c), (5, 1, to_x), (5, 2, to_xc)),
+            ((1, 3, to_y), (1, 4, to_a), (1, 5, to_ay)),
+            ((2, 6, to_z),),
+        )
+        return [sum_copy(1, *entry) for entry in plan[stage]]
+
+    def add_projected(stage):
+        for copy in projected_copies(stage):
+            copy.wait()
+        if stage == 2:
+            return sums[1, 2] + arrived[1, 6]
+        at = 3 * stage
+        sums[1, stage + 1] = (sums[1, stage] + arrived[1, at]) + (
+            arrived[1, at + 1] + arrived[1, at + 2]
+        )
+        for copy in projected_copies(stage + 1):
+            copy.start()
+
+    lax.fori_loop(0, STEPS - 1, step, 0)
+    last = STEPS - 1
+    slot = last % 2
     sums[0, 0] = gram(own[slot, p], own[slot, p])
-    own_projected = gram(own[slot, p], part[p])
-    cross.wait()
-    sums[0, 1] = own_projected + arrived[4, 0]
-    for stage, target in enumerate((to_c, to_y, to_a, to_b)):
-        copy = pltpu.make_async_remote_copy(
-            src_ref=sums.at[stage], dst_ref=arrived.at[stage], send_sem=g_send.at[stage],
-            recv_sem=g_recv.at[stage], device_id=target, device_id_type=MESH,
-        )
+    overlap_copy(0).start()
+    apply_matrix(
+        last, 0, True, False,
+        lambda stage: None if stage == 1 else add_overlap(min(stage, 1)),
+    )
+    apply_matrix(last, 1, True, False, lambda stage: add_overlap(2) if stage == 0 else None)
+    sums[1, 5] = gram(own[slot, 1 - p], part[1 - p])
+    sums[1, 0] = gram(own[slot, p], part[p])
+    for copy in projected_copies(0):
         copy.start()
-        copy.wait()
-        sums[stage + 1] = sums[stage] + arrived[stage]
-    gram_ref[...] = sums[4]
+    add_overlap(3)
+
+    lane = lax.broadcasted_iota(jnp.int32, (64, 128), 1)
+    diagonal = lane == lax.broadcasted_iota(jnp.int32, (64, 128), 0)
+    factor[0] = sums[0, 4]
+    factor[1] = jnp.where(diagonal, 1.0, 0.0)
+
+    def pivots(start, stop):
+        pl.when(row >= 0)(functools.partial(eliminate, factor, start, stop))
+
+    pivots(0, 22)
+    add_projected(0)
+    pivots(22, 44)
+    add_projected(1)
+    pivots(44, 64)
+    kept = jnp.where(diagonal, factor[0], 0.0)
+    whole = factor[1] / jnp.sqrt(jnp.sum(kept, axis=1, keepdims=True))
+    paired = jnp.concatenate([whole, turned(whole)], axis=0)
+
+    def against(left):
+        return lax.dot_general(
+            left, paired, (((1,), (1,)), ((), ())), precision=highest,
+            preferred_element_type=jnp.float32,
+        )
+
+    basis_ref[...] = scale * against(own[slot, p])
+    half = against(add_projected(2))
+    ritz_ref[...] = product(whole, jnp.concatenate([half, turned(half)], axis=0))
 
 
 def filtered(offsets, qpoints, lower_bound, upper_bound, force_constants, start_vectors):
@@ -461,12 +562,12 @@
     smem = pl.BlockSpec(memory_space=pltpu.SMEM)
     dma = pltpu.SemaphoreType.DMA
     single = jnp.float32
-    matrix = pltpu.VMEM((points, PIECES, 2, rows // PIECES, cols), jnp.bfloat16)
+    matrix = pltpu.VMEM((points, rows // TILE, 2, TILE, cols), jnp.bfloat16)
     return pl.pallas_call(
-        filter_kernel,
+        functools.partial(filter_kernel, math.sqrt(MODES)),
         out_shape=(
             jax.ShapeDtypeStruct((rows, 128), single),
-            jax.ShapeDtypeStruct((2, 64, 128), single),
+            jax.ShapeDtypeStruct((64, 128), single),
         ),
         in_specs=[smem] * 4 + [pl.BlockSpec(memory_space=pl.ANY), vmem],
         out_specs=(vmem, vmem),
@@ -481,18 +582,19 @@
             pltpu.VMEM((cols, 256), jnp.bfloat16),
             pltpu.VMEM((8, 128), single),
             pltpu.VMEM((8, 128), single),
-            pltpu.VMEM((6, 2, 64, 128), single),
-            pltpu.VMEM((5, 2, 64, 128), single),
+            pltpu.VMEM((2, 6, 64, 128), single),
+            pltpu.VMEM((2, 7, 64, 128), single),
+            pltpu.VMEM((2, 64, 128), single),
             dma((2,)),
             dma((points, KINDS)),
             dma((2, points, 2, PIECES, SUBS)),
             dma((2, points, PIECES, SUBS)),
             dma((2, points)),
-            dma((points, PIECES)),
-            dma((2, points, PIECES)),
+            dma((points, rows // TILE)),
+            dma((2, points, rows // TILE)),
             dma((2,)),
-            dma((5,)),
-            dma((5,)),
+            dma((2, 7)),
+            dma((2, 7)),
         ],
         compiler_params=pltpu.CompilerParams(
             collective_id=0, has_side_effects=True, vmem_limit_bytes=56 * 1024 * 1024
@@ -500,67 +602,10 @@
     )(offsets.T, qpoints, lower_bound, upper_bound, force_constants, start_vectors)
 
 
-def finish_kernel(scale, final_ref, gram_ref, basis_ref, ritz_ref):
-    size = gram_ref.shape[1]
-    tile = 8
-    gram = [gram_ref[0, t * tile:(t + 1) * tile, :] for t in range(size // tile)]
-    lane = lax.broadcasted_iota(jnp.int32, (tile, 128), 1)
-    line = lax.broadcasted_iota(jnp.int32, (tile, 128), 0)
-    inverse = [jnp.where(lane == line + t * tile, 1.0, 0.0) for t in range(size // tile)]
-    turn = sign_row(-1.0, 1.0)
-    for j in range(size):
-        home, at = j // tile, j % tile
-        row = gram[home][at:at + 1, :]
-        pivot = row[:, j:j + 1]
-        row = row / pivot
-        mate = inverse[home][at:at + 1, :] / pivot
-        row_turned = turn * pltpu.roll(row, 64, 1)
-        mate_turned = turn * pltpu.roll(mate, 64, 1)
-        for t in range(home, size // tile):
-            real = gram[t][:, j:j + 1]
-            imag = gram[t][:, 64 + j:65 + j]
-            if t == home:
-                below = line[:, :1] > at
-                real = jnp.where(below, real, 0.0)
-                imag = jnp.where(below, imag, 0.0)
-            gram[t] = gram[t] - (real * row + imag * row_turned)
-            inverse[t] = inverse[t] - (real * mate + imag * mate_turned)
-    scaled = []
-    for t in range(size // tile):
-        diagonal = jnp.sum(jnp.where(lane == line + t * tile, gram[t], 0.0), axis=1, keepdims=True)
-        scaled.append(inverse[t] / jnp.sqrt(diagonal))
-    whole = jnp.concatenate(scaled, axis=0)
-    paired = jnp.concatenate([whole, turn * pltpu.roll(whole, 64, 1)], axis=0)
-
-    def against(left):
-        return lax.dot_general(
-            left, paired, (((1,), (1,)), ((), ())), precision=highest,
-            preferred_element_type=jnp.float32,
-        )
-
-    basis_ref[...] = scale * against(final_ref[...])
-    half = against(gram_ref[1])
-    ritz_ref[...] = product(whole, jnp.concatenate([half, turn * pltpu.roll(half, 64, 1)], axis=0))
-
-
-def finish(final_pass, grams, modes):
-    vmem = pl.BlockSpec(memory_space=pltpu.VMEM)
-    return pl.pallas_call(
-        functools.partial(finish_kernel, math.sqrt(modes)),
-        out_shape=(
-            jax.ShapeDtypeStruct(final_pass.shape, jnp.float32),
-            jax.ShapeDtypeStruct(grams.shape[1:], jnp.float32),
-        ),
-        in_specs=[vmem] * 2,
-        out_specs=(vmem, vmem),
-    )(final_pass, grams)
-
-
 def on_block(force_constants, offsets, qpoints, lower_bound, upper_bound, start_vectors):
-    final_pass, grams = filtered(
+    basis_local, ritz_local = filtered(
         offsets, qpoints, lower_bound, upper_bound, force_constants, start_vectors
     )
-    basis_local, ritz_local = finish(final_pass, grams, MODES)
     return (basis_local[None], ritz_local[None])
 
 

time: 141 us -> 131 us (0.929)
  Pallas kernels: 139 us -> 126 us
  local copies, waits for them, and re-layouts: 0 us -> 2.95 us
    pallas_call x2 -> x1, Pallas kernels: 139 us -> 126 us  [filtered(): pl.pallas_call(functools.partial(filter_kernel, math.sqrt(MODES)), out_sh...]
    unnamed x0 -> x2, local copies, waits for them, and re-layouts: none -> 2.95 us
where the time goes in v3:
time: 131 us
  Pallas kernels  126 us (96%)
  local copies, waits for them, and re-layouts  2.95 us (2%)
  between operations  1.93 us (1%)
    pallas_call x1, Pallas kernels, filtered(): pl.pallas_call(functools.partial(filter_kernel, math.sqrt(MODES)), out_sh...  126 us
    unnamed x2, local copies, waits for them, and re-layouts  2.95 us

profile of v3, /device:TPU:0, one launch (start us, length us, event | category | flops | bytes accessed | tf_op | source)
XLA Modules:
  0.0 131.1 jit_solution(919330886875230749)
XLA Ops:
  1.9 126.2 %shard_map.77 = (f32[288,128]{1,0:T(8,128)}, f32[64,128]{1,0:T(8,128)}) custom-call(s32[3,9]{1,0:T(4,128)} %bitcast.5, s32[2,3]{1,0:T(2,128)} %qpoints_ref.1, f32[1]{0:T(128)S(6)} %copy.10.lower_ref, f32[1]{0:T(128)S(6)} %copy.11.upper_ref, f32[9,288,2304]{2,1,0:T(8,128)} %force_ref.1, f32[288,128]{1,0:T(8,128)} %start_ref.1), custom_call_target="tpu_custom_call" | custom-call | tf_op jit(solution)/shard_map/pallas_call | solution.py:566
  128.2 1.6 %copy.12 = f32[1,288,128]{2,1,0:T(8,128)} copy(f32[1,288,128]{2,1,0:T(8,128)} %bitcast.3) | data formatting | bytes 294912
  129.7 1.4 %copy.13 = f32[1,64,128]{2,1,0:T(8,128)} copy(f32[1,64,128]{2,1,0:T(8,128)} %bitcast.4) | data formatting | bytes 65536

commit v4 on v3

--- a/solution.py
+++ b/solution.py
@@ -180,8 +180,7 @@
 
 
 def filter_kernel(
-    scale,
-    offsets_ref, qpoints_ref, lower_ref, upper_ref, force_ref, start_ref, basis_ref, ritz_ref,
+    offsets_ref, qpoints_ref, lower_ref, upper_ref, force_ref, start_ref, final_ref, small_ref,
     tiles, high, low, full, own, part, other, split, bounds, partner_bounds, sums, arrived, factor,
     tile_sem, send_sem, level_recv, lane_recv, core_recv, x_send, x_recv, b_sem, g_send, g_recv,
 ):
@@ -208,13 +207,6 @@
     to_xc = (1 - p, row + 1 - 2 * c)
     to_ay = (p, row + 4 - 8 * level + 2 - 4 * y)
     to_z = (p, (opposite + level) * 4 + y * 2 + c)
-    to_far = [(group, (opposite + n) * 4 + y * 2 + c) for n in (0, 1)]
-
-    def guarded(condition, action):
-        if condition is True:
-            action()
-        elif condition is not False:
-            pl.when(condition)(action)
 
     def tile_copy(index, slot):
         where = pl.ds(pl.multiple_of(index * TILE, 8), TILE)
@@ -282,6 +274,7 @@
         return [piece * (depth // TILE) + n for n in range(0, depth // TILE, GROUP)]
 
     def direct(slot, q, piece, group_at):
+        to_far = [(group, (opposite + n) * 4 + y * 2 + c) for n in (0, 1)]
         count = SUBS * GROUP * TILE // depth
 
         @pl.when(far_piece == piece)
@@ -327,8 +320,7 @@
 
         lane = full.at[slot, q, :, y, c]
         send(lane, lane, q, ACROSS_Y, core_recv.at[slot, q], to_c).wait_send()
-        half = full.at[slot, q, :, :, c]
-        core_copy(slot, q, half).wait_send()
+        core_copy(slot, q, full.at[slot, q, :, :, c]).wait_send()
 
     def tile_rows(tile):
         return pl.ds(pl.multiple_of(tile * TILE, 8), GROUP * TILE)
@@ -341,11 +333,15 @@
             device_id=to_x, device_id_type=MESH,
         )
 
-    def divide(slot, q):
-        values = full[slot, q].reshape(cols, 128)
-        upper = values.astype(jnp.bfloat16)
-        split[:, :128] = upper
-        split[:, 128:] = (values - upper.astype(jnp.float32)).astype(jnp.bfloat16)
+    def divide(slot, q, core):
+        for at_level in (0, 1):
+            for yy in (0, 1):
+                values = full[slot, q, at_level, yy, core]
+                upper = values.astype(jnp.bfloat16)
+                index = at_level * 4 + yy * 2 + core
+                where = pl.ds(pl.multiple_of(index * rows, 16), rows)
+                split[where, :128] = upper
+                split[where, 128:] = (values - upper.astype(jnp.float32)).astype(jnp.bfloat16)
 
     def multiply(q, tile):
         def stacked(ref):
@@ -427,30 +423,34 @@
     lax.fori_loop(2 * third, 3 * third, assemble, 0)
     bound_copy.wait()
 
-    def apply_matrix(k, q, later, middle, extra=lambda stage: None):
+    def apply_matrix(k, q, extra):
         slot = k % 2
-        wanted = True if q == 0 else later
-        other_slot, ready = (slot, later) if q == 0 else (1 - slot, middle)
+        later = k > 0
+        middle = k < STEPS - 1
+        wanted = later | (q == 0)
+        other_slot = jnp.where(q == 0, slot, 1 - slot)
+        ready = jnp.where(q == 0, k > 0, k < STEPS - 1)
 
         def ahead(stage):
             for sub in AHEAD[stage]:
-                guarded(ready, functools.partial(lanes, other_slot, 1 - q, sub))
+                pl.when(ready)(functools.partial(lanes, other_slot, 1 - q, sub))
             extra(stage)
 
         def take():
+            divide(slot, q, c)
             collect(slot, q)
-            divide(slot, q)
-
-        guarded(wanted, functools.partial(relays, slot, q))
+            divide(slot, q, 1 - c)
+
+        pl.when(wanted)(functools.partial(relays, slot, q))
         ahead(0)
-        guarded(wanted, take)
+        pl.when(wanted)(take)
         for stage, piece in enumerate((1 - far_piece, far_piece)):
             for tile in tiles_of(piece):
-                guarded(later, partial_copy(1 - slot, q, tile).wait_send)
+                pl.when(later)(partial_copy(1 - slot, q, tile).wait_send)
                 multiply(q, tile)
-                guarded(middle, partial_copy(slot, q, tile).start)
+                pl.when(middle)(partial_copy(slot, q, tile).start)
             ahead(1 + stage)
-        guarded(wanted, functools.partial(await_sends, slot, q))
+        pl.when(wanted)(functools.partial(await_sends, slot, q))
 
     def advance(k, q):
         slot = k % 2
@@ -462,12 +462,6 @@
                 direct(1 - slot, q, piece, sub)
         near(1 - slot, q)
 
-    def step(k, carry):
-        for q in (0, 1):
-            apply_matrix(k, q, k > 0, True)
-            advance(k, q)
-        return carry
-
     def gram(left, right):
         whole = lax.dot_general(
             left, right, (((0,), (0,)), ((), ())), precision=highest,
@@ -511,18 +505,38 @@
         for copy in projected_copies(stage + 1):
             copy.start()
 
-    lax.fori_loop(0, STEPS - 1, step, 0)
-    last = STEPS - 1
-    slot = last % 2
-    sums[0, 0] = gram(own[slot, p], own[slot, p])
-    overlap_copy(0).start()
-    apply_matrix(
-        last, 0, True, False,
-        lambda stage: None if stage == 1 else add_overlap(min(stage, 1)),
-    )
-    apply_matrix(last, 1, True, False, lambda stage: add_overlap(2) if stage == 0 else None)
-    sums[1, 5] = gram(own[slot, 1 - p], part[1 - p])
-    sums[1, 0] = gram(own[slot, p], part[p])
+    slot = (STEPS - 1) % 2
+    first_final = 2 * (STEPS - 1)
+
+    def turn(index, carry):
+        k, q = index // 2, index % 2
+
+        @pl.when(index == first_final)
+        def _():
+            sums[0, 0] = gram(own[slot, p], own[slot, p])
+            overlap_copy(0).start()
+
+        def extra(stage):
+            for at_turn, at_stage, number in ((0, 0, 0), (0, 2, 1), (1, 0, 2)):
+                if stage == at_stage:
+                    pl.when(index == first_final + at_turn)(
+                        functools.partial(add_overlap, number)
+                    )
+
+        apply_matrix(k, q, extra)
+
+        @pl.when(k == STEPS - 1)
+        def _():
+            at = jnp.where(p == q, 0, 5)
+            sums[1, at] = gram(own[slot, q], part[q])
+
+        @pl.when(k < STEPS - 1)
+        def _():
+            advance(k, q)
+
+        return carry
+
+    lax.fori_loop(0, 2 * STEPS, turn, 0)
     for copy in projected_copies(0):
         copy.start()
     add_overlap(3)
@@ -541,18 +555,10 @@
     add_projected(1)
     pivots(44, 64)
     kept = jnp.where(diagonal, factor[0], 0.0)
-    whole = factor[1] / jnp.sqrt(jnp.sum(kept, axis=1, keepdims=True))
-    paired = jnp.concatenate([whole, turned(whole)], axis=0)
-
-    def against(left):
-        return lax.dot_general(
-            left, paired, (((1,), (1,)), ((), ())), precision=highest,
-            preferred_element_type=jnp.float32,
-        )
-
-    basis_ref[...] = scale * against(own[slot, p])
-    half = against(add_projected(2))
-    ritz_ref[...] = product(whole, jnp.concatenate([half, turned(half)], axis=0))
+    inverse = factor[1] / jnp.sqrt(jnp.sum(kept, axis=1, keepdims=True))
+    small_ref[0] = inverse
+    final_ref[...] = own[slot, p]
+    small_ref[1] = add_projected(2)
 
 
 def filtered(offsets, qpoints, lower_bound, upper_bound, force_constants, start_vectors):
@@ -564,10 +570,10 @@
     single = jnp.float32
     matrix = pltpu.VMEM((points, rows // TILE, 2, TILE, cols), jnp.bfloat16)
     return pl.pallas_call(
-        functools.partial(filter_kernel, math.sqrt(MODES)),
+        filter_kernel,
         out_shape=(
             jax.ShapeDtypeStruct((rows, 128), single),
-            jax.ShapeDtypeStruct((64, 128), single),
+            jax.ShapeDtypeStruct((2, 64, 128), single),
         ),
         in_specs=[smem] * 4 + [pl.BlockSpec(memory_space=pl.ANY), vmem],
         out_specs=(vmem, vmem),
@@ -602,10 +608,39 @@
     )(offsets.T, qpoints, lower_bound, upper_bound, force_constants, start_vectors)
 
 
+def finish_kernel(scale, final_ref, small_ref, basis_ref, ritz_ref):
+    inverse = small_ref[0]
+    paired = jnp.concatenate([inverse, turned(inverse)], axis=0)
+
+    def against(left):
+        return lax.dot_general(
+            left, paired, (((1,), (1,)), ((), ())), precision=highest,
+            preferred_element_type=jnp.float32,
+        )
+
+    basis_ref[...] = scale * against(final_ref[...])
+    half = against(small_ref[1])
+    ritz_ref[...] = product(inverse, jnp.concatenate([half, turned(half)], axis=0))
+
+
+def finish(final_pass, small):
+    vmem = pl.BlockSpec(memory_space=pltpu.VMEM)
+    return pl.pallas_call(
+        functools.partial(finish_kernel, math.sqrt(MODES)),
+        out_shape=(
+            jax.ShapeDtypeStruct(final_pass.shape, jnp.float32),
+            jax.ShapeDtypeStruct(small.shape[1:], jnp.float32),
+        ),
+        in_specs=[vmem] * 2,
+        out_specs=(vmem, vmem),
+    )(final_pass, small)
+
+
 def on_block(force_constants, offsets, qpoints, lower_bound, upper_bound, start_vectors):
-    basis_local, ritz_local = filtered(
+    final_pass, small = filtered(
         offsets, qpoints, lower_bound, upper_bound, force_constants, start_vectors
     )
+    basis_local, ritz_local = finish(final_pass, small)
     return (basis_local[None], ritz_local[None])
 
 

time: 131 us -> 130 us (level)
  local copies, waits for them, and re-layouts: 2.95 us -> 0 us
    unnamed x2 -> x0, local copies, waits for them, and re-layouts: 2.95 us -> none
    pallas_call x1 -> x2, Pallas kernels: 126 us -> 127 us  [the longest x1 125 us: filtered(): pl.pallas_call(filter_kernel, out_shape=(jax.ShapeDtypeStruct((rows, 128)...]
where the time goes in v4:
time: 130 us; the launch traced here: 129 us
  Pallas kernels  127 us (98%)
  between operations  1.93 us (1%)
    pallas_call x1, Pallas kernels, filtered(): pl.pallas_call(filter_kernel, out_shape=(jax.ShapeDtypeStruct((rows, 128)...  125 us

profile of v4, /device:TPU:0, one launch (start us, length us, event | category | flops | bytes accessed | tf_op | source)
XLA Modules:
  0.0 129.4 jit_solution(5976424902734609603)
XLA Ops:
  1.9 125.2 %shard_map.77 = (f32[288,128]{1,0:T(8,128)}, f32[2,64,128]{2,1,0:T(8,128)}) custom-call(s32[3,9]{1,0:T(4,128)} %bitcast.3, s32[2,3]{1,0:T(2,128)} %qpoints_ref.1, f32[1]{0:T(128)S(6)} %copy.8.lower_ref, f32[1]{0:T(128)S(6)} %copy.9.upper_ref, f32[9,288,2304]{2,1,0:T(8,128)} %force_ref.1, f32[288,128]{1,0:T(8,128)} %start_ref.1), custom_call_target="tpu_custom_call" | custom-call | tf_op jit(solution)/shard_map/pallas_call | solution.py:572
  127.1 2.3 %shard_map.78 = (f32[288,128]{1,0:T(8,128)}, f32[64,128]{1,0:T(8,128)}) custom-call(f32[288,128]{1,0:T(8,128)} %get-tuple-element.6.final_ref, f32[2,64,128]{2,1,0:T(8,128)} %get-tuple-element.7.small_ref), custom_call_target="tpu_custom_call" | custom-call | tf_op jit(solution)/shard_map/pallas_call | solution.py:628

commit v5 on v4

--- a/solution.py
+++ b/solution.py
@@ -125,8 +125,8 @@
 
 STEPS = 5
 PIECES = 2
-SUBS = 3
-AHEAD = ((0,), (1,), (2,))
+SUBS = 6
+AHEAD = ((0, 1), (2, 3), (4, 5))
 TILE = 48
 GROUP = 3
 FAR, NEAR, ACROSS_Y, ACROSS_C = 0, 1, 2, 3

time: 130 us -> 129 us (level)
  no operation moved by 1% of the time
where the time goes in v5:
time: 129 us
  Pallas kernels  127 us (98%)
  between operations  1.93 us (1%)
    pallas_call x1, Pallas kernels, filtered(): pl.pallas_call(filter_kernel, out_shape=(jax.ShapeDtypeStruct((rows, 128)...  125 us

profile of v5, /device:TPU:0, one launch (start us, length us, event | category | flops | bytes accessed | tf_op | source)
XLA Modules:
  0.0 129.0 jit_solution(497622300012294186)
XLA Ops:
  1.9 124.8 %shard_map.77 = (f32[288,128]{1,0:T(8,128)}, f32[2,64,128]{2,1,0:T(8,128)}) custom-call(s32[3,9]{1,0:T(4,128)} %bitcast.3, s32[2,3]{1,0:T(2,128)} %qpoints_ref.1, f32[1]{0:T(128)S(6)} %copy.8.lower_ref, f32[1]{0:T(128)S(6)} %copy.9.upper_ref, f32[9,288,2304]{2,1,0:T(8,128)} %force_ref.1, f32[288,128]{1,0:T(8,128)} %start_ref.1), custom_call_target="tpu_custom_call" | custom-call | tf_op jit(solution)/shard_map/pallas_call | solution.py:572
  126.7 2.3 %shard_map.78 = (f32[288,128]{1,0:T(8,128)}, f32[64,128]{1,0:T(8,128)}) custom-call(f32[288,128]{1,0:T(8,128)} %get-tuple-element.6.final_ref, f32[2,64,128]{2,1,0:T(8,128)} %get-tuple-element.7.small_ref), custom_call_target="tpu_custom_call" | custom-call | tf_op jit(solution)/shard_map/pallas_call | solution.py:628
